TPU v7x, 32 devices: a whole 2x2x4 slice. The times are simulated.
32 devices in a mesh: tm: 8 (over z, y), space: 4 (over x, core).
Axes of the slice: x: 2, y: 2, z: 4, core: 2. Of those that a mesh axis runs over, the one named last changes fastest.
Arguments:
- queries: bfloat16 [8, 16, 32, 768], P('tm', 'space')
- key_vectors: bfloat16 [8, 16, 32, 768], P('tm', 'space')
- values: bfloat16 [8, 16, 32, 768], P('tm', 'space'), may hold values from -6 to 6
- grad_out: bfloat16 [8, 16, 32, 768], P('tm', 'space'), may hold values from -6 to 6
- windows: int32 [2, 6], replicated, may hold values from 1 to 31, as said below
Outputs:
- attended: bfloat16 [8, 16, 32, 768], P('tm', 'space')
- grad_queries: bfloat16 [8, 16, 32, 768], P('tm', 'space')
- grad_keys: bfloat16 [8, 16, 32, 768], P('tm', 'space')
- value_gradient: bfloat16 [8, 16, 32, 768], P('tm', 'space')
Inputs may be any that keep to these rules, and one draw needn't show every extreme that they name: windows[0, h] is 1 to 2 and some head has 2; windows[1, h] is a quarter of 32 or more and some head has 31.
All inputs are finite; a program needn't handle non-finite values.
Results may differ from a plain program's by a relative error of at most 0.025.
Values may be sent and summed in bfloat16 or wider, within the bound.
A program may use at most 64 MiB of HBM per device.

v0:
```python
import math

import jax
import jax.numpy as jnp
from jax import lax
from jax.sharding import PartitionSpec as P

masked_score = -1e30


def padded(x, sides, width):
    for axis, dim in sides:
        peers, length = (lax.axis_size(axis), x.shape[dim])
        up = [(i, (i + 1) % peers) for i in range(peers - 1)]
        down = [(j, i) for i, j in up]
        last = lax.slice_in_dim(x, length - width, length, axis=dim)
        leading = lax.slice_in_dim(x, 0, width, axis=dim)
        before = lax.ppermute(last, axis, up)
        after = lax.ppermute(leading, axis, down)
        x = jnp.concatenate([before, x, after], axis=dim)
    return x


def from_behind(x, axis, by):
    peers = lax.axis_size(axis)
    pairs = [(i, i + by) for i in range(peers) if 0 <= i + by < peers]
    return lax.ppermute(x, axis, pairs)


def window_mask(
    windows, frame_index, block_index, row_extent, row_count, col_count, frame_total, row_sum_total
):
    query_count = row_count * col_count
    query_ids = jnp.arange(query_count, dtype=jnp.int32)
    query_row = query_ids // col_count
    query_col = query_ids % col_count
    near_rows = row_count + 2 * row_extent
    key_ids = jnp.arange(3 * near_rows * col_count, dtype=jnp.int32)
    key_frame = key_ids // (near_rows * col_count) - 1
    key_row = key_ids // col_count % near_rows - row_extent
    key_col = key_ids % col_count
    global_frame = frame_index + key_frame
    global_row = block_index * row_count + key_row
    inside = (
        (global_frame >= 0)
        & (global_frame < frame_total)
        & (global_row >= 0)
        & (global_row < row_sum_total)
    )
    row_gap = jnp.abs(query_row[:, None] - key_row[None, :])
    col_gap = jnp.abs(query_col[:, None] - key_col[None, :])
    return (
        inside[None, None, :]
        & (row_gap[None] <= windows[0][:, None, None])
        & (col_gap[None] <= windows[1][:, None, None])
    )


def on_device(queries, key_vectors, values, grad_out, windows):
    row_count = queries.shape[1]
    col_count = queries.shape[2]
    feature_count = queries.shape[3]
    head_count = windows.shape[1]
    head_size = feature_count // head_count
    row_extent = row_count // 2
    near_rows = row_count + 2 * row_extent
    score_scale = 1.0 / math.sqrt(head_size)
    local_shape = (1, row_count, col_count, feature_count)

    def as_blocks(array):
        return array.reshape(1, 2, row_extent, col_count, array.shape[-1])

    def by_head(array):
        return array.reshape(-1, head_count, head_size)

    in_window = window_mask(
        windows,
        lax.axis_index("tm"),
        lax.axis_index("space"),
        row_extent,
        row_count,
        col_count,
        lax.axis_size("tm"),
        row_count * lax.axis_size("space"),
    )
    near_keys, near_values = (
        padded(as_blocks(key_vectors), (("tm", 0), ("space", 1)), 1),
        padded(as_blocks(values), (("tm", 0), ("space", 1)), 1),
    )
    near_keys = by_head(near_keys)
    near_values = by_head(near_values)
    local_query = by_head(queries)
    local_grad = by_head(grad_out)
    scores = (
        jnp.einsum("qhd,khd->hqk", local_query, near_keys, preferred_element_type=jnp.float32)
        * score_scale
    )
    scores = jnp.where(in_window, scores, masked_score)
    row_top = jnp.max(scores, axis=2, keepdims=True)
    exp_total = jnp.sum(jnp.where(in_window, jnp.exp(scores - row_top), 0.0), axis=2, keepdims=True)
    log_total = row_top + jnp.log(exp_total)
    soft_weights = jnp.where(in_window, jnp.exp(scores - log_total), 0.0)
    weights_low = soft_weights.astype(jnp.bfloat16)
    attended = jnp.einsum(
        "hqk,khd->qhd", weights_low, near_values, preferred_element_type=jnp.float32
    ).astype(jnp.bfloat16)
    out_dot = jnp.einsum("qhd,qhd->hq", local_grad, attended, preferred_element_type=jnp.float32)
    grad_weights = jnp.einsum(
        "qhd,khd->hqk", local_grad, near_values, preferred_element_type=jnp.float32
    )
    grad_scores = (soft_weights * (grad_weights - out_dot[:, :, None])).astype(jnp.bfloat16)
    grad_query = (
        jnp.einsum("hqk,khd->qhd", grad_scores, near_keys, preferred_element_type=jnp.float32)
        * score_scale
    ).astype(jnp.bfloat16)
    part_shape = (3, near_rows, col_count, feature_count)
    part_keys = (
        jnp.einsum("hqk,qhd->khd", grad_scores, local_query, preferred_element_type=jnp.float32)
        * score_scale
    ).reshape(part_shape)
    partial_value_rows = jnp.einsum(
        "hqk,qhd->khd", weights_low, local_grad, preferred_element_type=jnp.float32
    ).reshape(part_shape)
    centre_keys = part_keys[:, row_extent : row_extent + row_count]
    centre_values = partial_value_rows[:, row_extent : row_extent + row_count]
    for offset in (1, -1):
        rim_start = row_extent + row_count if offset == 1 else 0
        land_at = 0 if offset == 1 else row_count - row_extent
        got_keys, got_values = from_behind(
            (
                part_keys[:, rim_start : rim_start + row_extent],
                partial_value_rows[:, rim_start : rim_start + row_extent],
            ),
            "space",
            offset,
        )
        centre_keys = centre_keys.at[:, land_at : land_at + row_extent].add(got_keys)
        centre_values = centre_values.at[:, land_at : land_at + row_extent].add(got_values)
    own_keys = centre_keys[1:2]
    own_values = centre_values[1:2]
    for offset in (1, -1):
        rim_frame = 2 if offset == 1 else 0
        got_keys, got_values = from_behind(
            (centre_keys[rim_frame : rim_frame + 1], centre_values[rim_frame : rim_frame + 1]),
            "tm",
            offset,
        )
        own_keys = own_keys + got_keys
        own_values = own_values + got_values
    grad_keys = own_keys.astype(jnp.bfloat16)
    value_gradient = own_values.astype(jnp.bfloat16)
    return (
        attended.reshape(local_shape),
        grad_query.reshape(local_shape),
        grad_keys,
        value_gradient,
    )


def solution(mesh):
    in_specs = (
        P("tm", "space", None, None),
        P("tm", "space", None, None),
        P("tm", "space", None, None),
        P("tm", "space", None, None),
        P(),
    )
    out_specs = (
        P("tm", "space", None, None),
        P("tm", "space", None, None),
        P("tm", "space", None, None),
        P("tm", "space", None, None),
    )
    return jax.shard_map(
        on_device, mesh=mesh, in_specs=in_specs, out_specs=out_specs, check_vma=False
    )
```

profile of v0, /device:TPU:5, one launch (start us, length us, event | category | flops | bytes accessed | tf_op | source)
XLA Modules:
  0.0 121.9 jit_solution(6942684536729590248)
XLA Ops:
  0.6 2.1 %collective-permute-start.5 = (bf16[1,2,2,32,768]{4,3,2,1,0:T(8,128)(2,1)}, bf16[1,2,2,32,768]{4,3,2,1,0:T(8,128)(2,1)S(1)}, u32[]{:S(2)}, u32[]{:S(2)}) collective-permute-start(bf16[1,2,2,32,768]{4,3,2,1,0:T(8,128)(2,1)} %bitcast.50), channel_id=1, source_target_pairs={{4,0},{8,4},{12,8},{16,12},{20,16},{24,20},{28,24},{5,1},{9,5},{13... | collective-permute-start | bytes 589832 | tf_op jit(solution)/shard_map/ppermute | solution.py:19
  2.7 4.3 %collective-permute-start.4 = (bf16[1,2,2,32,768]{4,3,2,1,0:T(8,128)(2,1)}, bf16[1,2,2,32,768]{4,3,2,1,0:T(8,128)(2,1)S(1)}, u32[]{:S(2)}, u32[]{:S(2)}) collective-permute-start(bf16[1,2,2,32,768]{4,3,2,1,0:T(8,128)(2,1)} %bitcast.51), channel_id=1, source_target_pairs={{0,4},{4,8},{8,12},{12,16},{16,20},{20,24},{24,28},{1,5},{5,9},{9,... | collective-permute-start | bytes 589832 | tf_op jit(solution)/shard_map/ppermute | solution.py:18
  7.0 1.9 %collective-permute-start.1 = (bf16[1,2,2,32,768]{4,3,2,1,0:T(8,128)(2,1)}, bf16[1,2,2,32,768]{4,3,2,1,0:T(8,128)(2,1)S(1)}, u32[]{:S(2)}, u32[]{:S(2)}) collective-permute-start(bf16[1,2,2,32,768]{4,3,2,1,0:T(8,128)(2,1)} %bitcast.54), channel_id=1, source_target_pairs={{4,0},{8,4},{12,8},{16,12},{20,16},{24,20},{28,24},{5,1},{9,5},{13... | collective-permute-start | bytes 589832 | tf_op jit(solution)/shard_map/ppermute | solution.py:19
  8.9 4.3 %collective-permute-start = (bf16[1,2,2,32,768]{4,3,2,1,0:T(8,128)(2,1)}, bf16[1,2,2,32,768]{4,3,2,1,0:T(8,128)(2,1)S(1)}, u32[]{:S(2)}, u32[]{:S(2)}) collective-permute-start(bf16[1,2,2,32,768]{4,3,2,1,0:T(8,128)(2,1)} %bitcast.55), channel_id=1, source_target_pairs={{0,4},{4,8},{8,12},{12,16},{16,20},{20,24},{24,28},{1,5},{5,9},{9,... | collective-permute-start | bytes 589832 | tf_op jit(solution)/shard_map/ppermute | solution.py:18
  13.2 1.9 %reshape.345 = bf16[128,6,128]{2,1,0:T(8,128)(2,1)} reshape(bf16[1,4,32,768]{3,2,1,0:T(8,128)(2,1)} %param.13) | data formatting | bytes 393216 | tf_op jit(solution)/shard_map/reshape | solution.py:74
  15.1 1.9 %reshape.347 = bf16[128,6,128]{2,1,0:T(8,128)(2,1)} reshape(bf16[1,4,32,768]{3,2,1,0:T(8,128)(2,1)} %param.16) | data formatting | bytes 393216 | tf_op jit(solution)/shard_map/reshape | solution.py:74
  17.0 0.2 subtract_abs_fusion
  17.2 0.2 subtract_abs_fusion.1
  17.4 0.8 slice_bitcast_fusion.1
  18.2 0.9 collective-permute-done.4
  19.0 1.0 pad_maximum_fusion.3
  20.1 2.9 %collective-permute-start.7 = (bf16[3,1,2,32,768]{4,3,2,1,0:T(8,128)(2,1)S(1)}, bf16[3,1,2,32,768]{4,3,2,1,0:T(8,128)(2,1)S(1)}, u32[]{:S(2)}, u32[]{:S(2)}) collective-permute-start(bf16[3,1,2,32,768]{4,3,2,1,0:T(8,128)(2,1)S(1)} %get-tuple-element.65), channel_id=1, source_target_pairs={{1,0},{2,1},{3,2},{5,4},{6,5},{7,6},{9,8},{10,9},{11,10},{13,12},{... | collective-permute-start | bytes 884744 | tf_op jit(solution)/shard_map/ppermute | solution.py:19
  23.0 3.0 %collective-permute-start.6 = (bf16[3,1,2,32,768]{4,3,2,1,0:T(8,128)(2,1)S(1)}, bf16[3,1,2,32,768]{4,3,2,1,0:T(8,128)(2,1)S(1)}, u32[]{:S(2)}, u32[]{:S(2)}) collective-permute-start(bf16[3,1,2,32,768]{4,3,2,1,0:T(8,128)(2,1)S(1)} %get-tuple-element.64), channel_id=1, source_target_pairs={{0,1},{1,2},{2,3},{4,5},{5,6},{6,7},{8,9},{9,10},{10,11},{12,13},{... | collective-permute-start | bytes 884744 | tf_op jit(solution)/shard_map/ppermute | solution.py:18
  26.1 0.1 pad_maximum_fusion.2
  26.1 0.9 fusion.43
  27.0 1.9 %collective-permute-start.3 = (bf16[3,1,2,32,768]{4,3,2,1,0:T(8,128)(2,1)}, bf16[3,1,2,32,768]{4,3,2,1,0:T(8,128)(2,1)}, u32[]{:S(2)}, u32[]{:S(2)}) collective-permute-start(bf16[3,1,2,32,768]{4,3,2,1,0:T(8,128)(2,1)} %get-tuple-element.67), channel_id=1, source_target_pairs={{1,0},{2,1},{3,2},{5,4},{6,5},{7,6},{9,8},{10,9},{11,10},{13,12},{... | collective-permute-start | bytes 884744 | tf_op jit(solution)/shard_map/ppermute | solution.py:19
  28.9 3.6 %collective-permute-start.2 = (bf16[3,1,2,32,768]{4,3,2,1,0:T(8,128)(2,1)}, bf16[3,1,2,32,768]{4,3,2,1,0:T(8,128)(2,1)}, u32[]{:S(2)}, u32[]{:S(2)}) collective-permute-start(bf16[3,1,2,32,768]{4,3,2,1,0:T(8,128)(2,1)} %get-tuple-element.66), channel_id=1, source_target_pairs={{0,1},{1,2},{2,3},{4,5},{5,6},{6,7},{8,9},{9,10},{10,11},{12,13},{... | collective-permute-start | bytes 884744 | tf_op jit(solution)/shard_map/ppermute | solution.py:18
  32.6 0.2 pad_maximum_fusion.1
  32.8 1.4 %reshape.344 = bf16[768,6,128]{2,1,0:T(8,128)(2,1)S(1)} reshape(bf16[3,4,2,32,768]{4,3,2,1,0:T(8,128)(2,1)S(1)} %pad_maximum_fusion.1) | data formatting | bytes 2359296 | tf_op jit(solution)/shard_map/reshape | solution.py:74
  34.2 1.0 copy.29
  35.2 2.3 %fusion.1 = (f32[6,128]{1,0:T(8,128)S(1)}, f32[6,768,128]{2,1,0:T(8,128)S(1)}) fusion(s32[6]{0:T(128)S(1)} %get-tuple-element.69, s32[128,768]{0,1:T(8,128)S(1)} %subtract_abs_fusion, s32[6]{0:T(128)S(1)} %get-tuple-element.68, s32[128,768]{0,1:T(8,128)S(1)} %subtract_abs_fusion.1, pred[768]{0:T(1024)(128)(4,1)S(1)} %fusion.35, ...), kind=kOutput, calls=%fused_computation.7 | convolution fusion | flops 155122944 | bytes 4525872 | tf_op jit(solution)/shard_map/qhd,khd->hqk/dot_general | solution.py:95
  37.6 1.1 select_reduce_fusion
  38.8 0.2 copy-done.8
  39.0 0.3 copy-done.23
  39.4 1.4 %pad_maximum_fusion = bf16[3,4,2,32,768]{4,3,2,1,0:T(8,128)(2,1)S(1)} fusion(bf16[3,1,2,32,768]{4,3,2,1,0:T(8,128)(2,1)} %collective-permute-done.3, bf16[1,2,2,32,768]{4,3,2,1,0:T(8,128)(2,1)S(1)} %copy-done.21, bf16[1,2,2,32,768]{4,3,2,1,0:T(8,128)(2,1)S(1)} %bitcast.57, bf16[1,2,2,32,768]{4,3,2,1,0:T(8,128)(2,1)S(1)} %copy-done.23, ...), kind=kLoop, calls=%fused_computation.11 | loop fusion | flops 2359296 | bytes 2359296 | tf_op jit(solution)/shard_map/concatenate | solution.py:20
  40.7 2.2 %reshape.342 = bf16[768,6,128]{2,1,0:T(8,128)(2,1)} reshape(bf16[3,4,2,32,768]{4,3,2,1,0:T(8,128)(2,1)S(1)} %pad_maximum_fusion) | data formatting | bytes 2359296 | tf_op jit(solution)/shard_map/reshape | solution.py:74
  43.0 3.9 %bitcast_convert_fusion = (f32[6,128,128]{1,2,0:T(8,128)}, bf16[6,128,128]{2,1,0:T(8,128)(2,1)}) fusion(f32[6,768,128]{2,1,0:T(8,128)S(1)} %copy-done.9, f32[6,128]{1,0:T(8,128)S(1)} %log_add_fusion, s32[6]{0:T(128)S(1)} %get-tuple-element.69, s32[128,768]{0,1:T(8,128)} %copy-done.11, s32[6]{0:T(128)S(1)} %get-tuple-element.68, s32[128,768]{0,1:T(8,128)} %copy-done.14, ...), kind=kOutput, calls=%fused_computation.37 | convolution fusion | flops 156499968 | bytes 4919088 | tf_op jit(solution)/shard_map/hqk,khd->qhd/dot_general | solution.py:104
  46.9 1.2 %copy.42 = f32[6,128,128]{2,0,1:T(8,128)S(1)} copy(f32[6,128,128]{1,2,0:T(8,128)} %get-tuple-element.72) | data formatting | bytes 786432
  48.1 0.8 multiply_reduce_fusion
  49.0 0.9 copy.43
  49.9 3.0 %fusion = bf16[6,128,768]{1,2,0:T(8,128)(2,1)S(1)} fusion(f32[6,768,128]{2,1,0:T(8,128)S(1)} %copy-done.9, f32[6,128]{1,0:T(8,128)S(1)} %copy.43, f32[6,128]{1,0:T(8,128)S(1)} %log_add_fusion, bf16[768,6,128]{2,1,0:T(8,128)(2,1)} %reshape.342, bf16[128,6,128]{2,1,0:T(8,128)(2,1)S(1)} %copy-done.15, s32[6]{0:T(128)S(1)} %get-tuple-element.69, ...), kind=kOutput, calls=%fused_computation.1 | convolution fusion | flops 157483008 | bytes 5708592 | tf_op jit(solution)/shard_map/qhd,khd->hqk/dot_general | solution.py:108
  52.9 1.0 copy-done.4
  53.9 0.5 multiply_bitcast_fusion
  54.3 1.4 %copy.33 = f32[768,6,128]{2,1,0:T(8,128)S(1)} copy(f32[768,6,128]{2,0,1:T(8,128)S(1)} %multiply_bitcast_fusion) | data formatting | bytes 4718592 | tf_op jit(solution)/shard_map/mul | solution.py:118
  55.8 1.7 %reshape.349 = f32[3,8,32,768]{3,2,1,0:T(8,128)} reshape(f32[768,6,128]{2,1,0:T(8,128)S(1)} %copy.33) | data formatting | bytes 4718592 | tf_op jit(solution)/shard_map/reshape | solution.py:120
  57.5 2.5 %fusion.39 = (f32[3,2,32,768]{3,2,1,0:T(8,128)}, f32[3,2,32,768]{3,2,1,0:T(8,128)}) fusion(f32[3,8,32,768]{3,2,1,0:T(8,128)} %reshape.349), kind=kLoop, calls=%fused_computation.79 | loop fusion | bytes 2359296 | tf_op jit(solution)/shard_map/slice | solution.py:131
  60.0 1.9 %collective-permute-start.8 = (f32[3,2,32,768]{3,2,1,0:T(8,128)}, f32[3,2,32,768]{3,2,1,0:T(8,128)}, u32[]{:S(2)}, u32[]{:S(2)}) collective-permute-start(f32[3,2,32,768]{3,2,1,0:T(8,128)} %get-tuple-element.59), channel_id=1, source_target_pairs={{0,1},{1,2},{2,3},{4,5},{5,6},{6,7},{8,9},{9,10},{10,11},{12,13},{... | collective-permute-start | bytes 1769480 | tf_op jit(solution)/shard_map/ppermute | solution.py:27
  62.0 3.4 %collective-permute-start.9 = (f32[3,2,32,768]{3,2,1,0:T(8,128)}, f32[3,2,32,768]{3,2,1,0:T(8,128)}, u32[]{:S(2)}, u32[]{:S(2)}) collective-permute-start(f32[3,2,32,768]{3,2,1,0:T(8,128)} %get-tuple-element.58), channel_id=1, source_target_pairs={{1,0},{2,1},{3,2},{5,4},{6,5},{7,6},{9,8},{10,9},{11,10},{13,12},{... | collective-permute-start | bytes 1769480 | tf_op jit(solution)/shard_map/ppermute | solution.py:27
  65.4 2.2 %convolution_bitcast_fusion = f32[768,6,128]{2,0,1:T(8,128)S(1)} fusion(bf16[128,6,128]{2,1,0:T(8,128)(2,1)} %reshape.347, f32[6,768,128]{2,1,0:T(8,128)S(1)} %copy-done.10, f32[6,128]{1,0:T(8,128)S(1)} %log_add_fusion, s32[128,768]{0,1:T(8,128)S(1)} %copy-done.13, s32[128,768]{0,1:T(8,128)} %copy-done.14, s32[6]{0:T(128)S(1)} %get-tuple-element.69, ...), kind=kOutput, calls=%fused_computation.8 | convolution fusion | flops 156303360 | bytes 5705520 | tf_op jit(solution)/shard_map/hqk,qhd->khd/dot_general | solution.py:121
  67.6 1.4 %copy.35 = f32[768,6,128]{2,1,0:T(8,128)S(1)} copy(f32[768,6,128]{2,0,1:T(8,128)S(1)} %convolution_bitcast_fusion) | data formatting | bytes 4718592 | tf_op jit(solution)/shard_map/hqk,qhd->khd/transpose | solution.py:121
  69.0 1.7 %reshape.350 = f32[3,8,32,768]{3,2,1,0:T(8,128)} reshape(f32[768,6,128]{2,1,0:T(8,128)S(1)} %copy.35) | data formatting | bytes 4718592 | tf_op jit(solution)/shard_map/reshape | solution.py:123
  70.8 1.7 %copy-done = f32[3,8,32,768]{3,2,1,0:T(8,128)S(1)} copy-done((f32[3,8,32,768]{3,2,1,0:T(8,128)S(1)}, f32[3,8,32,768]{3,2,1,0:T(8,128)}, u32[]{:S(2)}) %copy-start) | copy-done | bytes 2359320
  72.4 0.1 fusion.38
  72.5 2.4 %collective-permute-start.12 = (f32[3,2,32,768]{3,2,1,0:T(8,128)S(1)}, f32[3,2,32,768]{3,2,1,0:T(8,128)S(1)}, u32[]{:S(2)}, u32[]{:S(2)}) collective-permute-start(f32[3,2,32,768]{3,2,1,0:T(8,128)S(1)} %get-tuple-element.57), channel_id=1, source_target_pairs={{0,1},{1,2},{2,3},{4,5},{5,6},{6,7},{8,9},{9,10},{10,11},{12,13},{... | collective-permute-start | bytes 1769480 | tf_op jit(solution)/shard_map/ppermute | solution.py:27
  74.9 2.3 %collective-permute-start.13 = (f32[3,2,32,768]{3,2,1,0:T(8,128)S(1)}, f32[3,2,32,768]{3,2,1,0:T(8,128)S(1)}, u32[]{:S(2)}, u32[]{:S(2)}) collective-permute-start(f32[3,2,32,768]{3,2,1,0:T(8,128)S(1)} %get-tuple-element.56), channel_id=1, source_target_pairs={{1,0},{2,1},{3,2},{5,4},{6,5},{7,6},{9,8},{10,9},{11,10},{13,12},{... | collective-permute-start | bytes 1769480 | tf_op jit(solution)/shard_map/ppermute | solution.py:27
  77.2 1.3 %fusion.10 = f32[3,4,32,768]{3,2,1,0:T(8,128)S(1)} fusion(f32[3,4,32,768]{3,2,1,0:T(8,128)S(1)} %slice-done.1, f32[3,2,32,768]{3,2,1,0:T(8,128)} %collective-permute-done.8, f32[3,8,32,768]{3,2,1,0:T(8,128)} %reshape.349), kind=kLoop, calls=%fused_computation.25 | loop fusion | flops 147456 | bytes 1769472 | tf_op jit(solution)/shard_map/scatter-add | solution.py:137
  78.5 1.2 fusion.9
  79.8 1.0 fusion.41
  80.8 1.9 %collective-permute-start.11 = (f32[1,4,32,768]{3,2,1,0:T(8,128)}, f32[1,4,32,768]{3,2,1,0:T(8,128)}, u32[]{:S(2)}, u32[]{:S(2)}) collective-permute-start(f32[1,4,32,768]{3,2,1,0:T(8,128)} %get-tuple-element.63), channel_id=1, source_target_pairs={{4,0},{8,4},{12,8},{16,12},{20,16},{24,20},{28,24},{5,1},{9,5},{13... | collective-permute-start | bytes 1179656 | tf_op jit(solution)/shard_map/ppermute | solution.py:27
  82.8 4.4 %collective-permute-start.10 = (f32[1,4,32,768]{3,2,1,0:T(8,128)}, f32[1,4,32,768]{3,2,1,0:T(8,128)}, u32[]{:S(2)}, u32[]{:S(2)}) collective-permute-start(f32[1,4,32,768]{3,2,1,0:T(8,128)} %get-tuple-element.62), channel_id=1, source_target_pairs={{0,4},{4,8},{8,12},{12,16},{16,20},{20,24},{24,28},{1,5},{5,9},{9,... | collective-permute-start | bytes 1179656 | tf_op jit(solution)/shard_map/ppermute | solution.py:27
  87.2 0.1 fusion.8
  87.3 0.1 fusion.7
  87.4 1.0 fusion.40
  88.4 2.0 %collective-permute-start.15 = (f32[1,4,32,768]{3,2,1,0:T(8,128)}, f32[1,4,32,768]{3,2,1,0:T(8,128)S(1)}, u32[]{:S(2)}, u32[]{:S(2)}) collective-permute-start(f32[1,4,32,768]{3,2,1,0:T(8,128)} %get-tuple-element.61), channel_id=1, source_target_pairs={{4,0},{8,4},{12,8},{16,12},{20,16},{24,20},{28,24},{5,1},{9,5},{13... | collective-permute-start | bytes 1179656 | tf_op jit(solution)/shard_map/ppermute | solution.py:27
  90.5 4.3 %collective-permute-start.14 = (f32[1,4,32,768]{3,2,1,0:T(8,128)}, f32[1,4,32,768]{3,2,1,0:T(8,128)}, u32[]{:S(2)}, u32[]{:S(2)}) collective-permute-start(f32[1,4,32,768]{3,2,1,0:T(8,128)} %get-tuple-element.60), channel_id=1, source_target_pairs={{0,4},{4,8},{8,12},{12,16},{16,20},{20,24},{24,28},{1,5},{5,9},{9,... | collective-permute-start | bytes 1179656 | tf_op jit(solution)/shard_map/ppermute | solution.py:27
  94.7 0.5 fusion.4
  95.2 0.2 copy.26
  95.4 0.9 reshape.346
  96.3 0.2 copy.31
  96.5 0.9 reshape.348
  97.5 14.3 %collective-permute-done.10 = f32[1,4,32,768]{3,2,1,0:T(8,128)} collective-permute-done((f32[1,4,32,768]{3,2,1,0:T(8,128)}, f32[1,4,32,768]{3,2,1,0:T(8,128)}, u32[]{:S(2)}, u32[]{:S(2)}) %collective-permute-start.10) | collective-permute-done | bytes 393248 | tf_op jit(solution)/shard_map/ppermute | solution.py:27
  111.8 1.8 %fusion.14 = bf16[1,4,32,768]{3,2,1,0:T(8,128)(2,1)} fusion(f32[1,4,32,768]{3,2,1,0:T(8,128)} %collective-permute-done.11, f32[1,4,32,768]{3,2,1,0:T(8,128)} %collective-permute-done.10, f32[3,4,32,768]{3,2,1,0:T(8,128)S(1)} %copy-done.3), kind=kLoop, calls=%fused_computation.34 | loop fusion | flops 294912 | bytes 1376256 | tf_op jit(solution)/shard_map/convert_element_type | solution.py:150
  113.6 6.6 %collective-permute-done.14 = f32[1,4,32,768]{3,2,1,0:T(8,128)} collective-permute-done((f32[1,4,32,768]{3,2,1,0:T(8,128)}, f32[1,4,32,768]{3,2,1,0:T(8,128)}, u32[]{:S(2)}, u32[]{:S(2)}) %collective-permute-start.14) | collective-permute-done | bytes 393248 | tf_op jit(solution)/shard_map/ppermute | solution.py:27
  120.2 1.7 %fusion.12 = bf16[1,4,32,768]{3,2,1,0:T(8,128)(2,1)} fusion(f32[1,4,32,768]{3,2,1,0:T(8,128)S(1)} %collective-permute-done.15, f32[1,4,32,768]{3,2,1,0:T(8,128)} %collective-permute-done.14, f32[3,4,32,768]{3,2,1,0:T(8,128)S(1)} %fusion.7), kind=kLoop, calls=%fused_computation.31 | loop fusion | flops 294912 | bytes 1376256 | tf_op jit(solution)/shard_map/convert_element_type | solution.py:151
  (69 shorter events, 0.3 us)
Async XLA Ops:
  0.6 25.4 %copy-start.18 = (bf16[1,4,32,768]{3,2,1,0:T(8,128)(2,1)S(1)}, bf16[1,4,32,768]{3,2,1,0:T(8,128)(2,1)}, u32[]{:S(2)}) copy-start(bf16[1,4,32,768]{3,2,1,0:T(8,128)(2,1)} %param.15) | copy-start | bytes 589828
  0.6 17.5 %collective-permute-start.5 = (bf16[1,2,2,32,768]{4,3,2,1,0:T(8,128)(2,1)}, bf16[1,2,2,32,768]{4,3,2,1,0:T(8,128)(2,1)S(1)}, u32[]{:S(2)}, u32[]{:S(2)}) collective-permute-start(bf16[1,2,2,32,768]{4,3,2,1,0:T(8,128)(2,1)} %bitcast.50), channel_id=1, source_target_pairs={{4,0},{8,4},{12,8},{16,12},{20,16},{24,20},{28,24},{5,1},{9,5},{13... | collective-permute-start | bytes 589832 | tf_op jit(solution)/shard_map/ppermute | solution.py:19
  2.7 16.3 %collective-permute-start.4 = (bf16[1,2,2,32,768]{4,3,2,1,0:T(8,128)(2,1)}, bf16[1,2,2,32,768]{4,3,2,1,0:T(8,128)(2,1)S(1)}, u32[]{:S(2)}, u32[]{:S(2)}) collective-permute-start(bf16[1,2,2,32,768]{4,3,2,1,0:T(8,128)(2,1)} %bitcast.51), channel_id=1, source_target_pairs={{0,4},{4,8},{8,12},{12,16},{16,20},{20,24},{24,28},{1,5},{5,9},{9,... | collective-permute-start | bytes 589832 | tf_op jit(solution)/shard_map/ppermute | solution.py:18
  7.0 19.0 %collective-permute-start.1 = (bf16[1,2,2,32,768]{4,3,2,1,0:T(8,128)(2,1)}, bf16[1,2,2,32,768]{4,3,2,1,0:T(8,128)(2,1)S(1)}, u32[]{:S(2)}, u32[]{:S(2)}) collective-permute-start(bf16[1,2,2,32,768]{4,3,2,1,0:T(8,128)(2,1)} %bitcast.54), channel_id=1, source_target_pairs={{4,0},{8,4},{12,8},{16,12},{20,16},{24,20},{28,24},{5,1},{9,5},{13... | collective-permute-start | bytes 589832 | tf_op jit(solution)/shard_map/ppermute | solution.py:19
  8.9 17.1 %collective-permute-start = (bf16[1,2,2,32,768]{4,3,2,1,0:T(8,128)(2,1)}, bf16[1,2,2,32,768]{4,3,2,1,0:T(8,128)(2,1)S(1)}, u32[]{:S(2)}, u32[]{:S(2)}) collective-permute-start(bf16[1,2,2,32,768]{4,3,2,1,0:T(8,128)(2,1)} %bitcast.55), channel_id=1, source_target_pairs={{0,4},{4,8},{8,12},{12,16},{16,20},{20,24},{24,28},{1,5},{5,9},{9,... | collective-permute-start | bytes 589832 | tf_op jit(solution)/shard_map/ppermute | solution.py:18
  17.2 20.4 %copy-start.11 = (s32[128,768]{0,1:T(8,128)}, s32[128,768]{0,1:T(8,128)S(1)}, u32[]{:S(2)}) copy-start(s32[128,768]{0,1:T(8,128)S(1)} %subtract_abs_fusion) | copy-start | bytes 1179652
  17.3 20.3 %copy-start.14 = (s32[128,768]{0,1:T(8,128)}, s32[128,768]{0,1:T(8,128)S(1)}, u32[]{:S(2)}) copy-start(s32[128,768]{0,1:T(8,128)S(1)} %subtract_abs_fusion.1) | copy-start | bytes 1179652
  18.2 14.5 %copy-start.17 = (bf16[1,4,32,768]{3,2,1,0:T(8,128)(2,1)S(1)}, bf16[1,4,32,768]{3,2,1,0:T(8,128)(2,1)}, u32[]{:S(2)}) copy-start(bf16[1,4,32,768]{3,2,1,0:T(8,128)(2,1)} %param.14) | copy-start | bytes 589828
  20.1 12.5 %collective-permute-start.7 = (bf16[3,1,2,32,768]{4,3,2,1,0:T(8,128)(2,1)S(1)}, bf16[3,1,2,32,768]{4,3,2,1,0:T(8,128)(2,1)S(1)}, u32[]{:S(2)}, u32[]{:S(2)}) collective-permute-start(bf16[3,1,2,32,768]{4,3,2,1,0:T(8,128)(2,1)S(1)} %get-tuple-element.65), channel_id=1, source_target_pairs={{1,0},{2,1},{3,2},{5,4},{6,5},{7,6},{9,8},{10,9},{11,10},{13,12},{... | collective-permute-start | bytes 884744 | tf_op jit(solution)/shard_map/ppermute | solution.py:19
  23.0 9.6 %collective-permute-start.6 = (bf16[3,1,2,32,768]{4,3,2,1,0:T(8,128)(2,1)S(1)}, bf16[3,1,2,32,768]{4,3,2,1,0:T(8,128)(2,1)S(1)}, u32[]{:S(2)}, u32[]{:S(2)}) collective-permute-start(bf16[3,1,2,32,768]{4,3,2,1,0:T(8,128)(2,1)S(1)} %get-tuple-element.64), channel_id=1, source_target_pairs={{0,1},{1,2},{2,3},{4,5},{5,6},{6,7},{8,9},{9,10},{10,11},{12,13},{... | collective-permute-start | bytes 884744 | tf_op jit(solution)/shard_map/ppermute | solution.py:18
  26.0 6.6 %copy-start.20 = (bf16[1,2,2,32,768]{4,3,2,1,0:T(8,128)(2,1)}, bf16[1,2,2,32,768]{4,3,2,1,0:T(8,128)(2,1)S(1)}, u32[]{:S(2)}) copy-start(bf16[1,2,2,32,768]{4,3,2,1,0:T(8,128)(2,1)S(1)} %collective-permute-done.1) | copy-start | bytes 589828
  26.1 6.6 %copy-start.22 = (bf16[1,2,2,32,768]{4,3,2,1,0:T(8,128)(2,1)}, bf16[1,2,2,32,768]{4,3,2,1,0:T(8,128)(2,1)S(1)}, u32[]{:S(2)}) copy-start(bf16[1,2,2,32,768]{4,3,2,1,0:T(8,128)(2,1)S(1)} %collective-permute-done) | copy-start | bytes 589828
  27.0 11.8 %collective-permute-start.3 = (bf16[3,1,2,32,768]{4,3,2,1,0:T(8,128)(2,1)}, bf16[3,1,2,32,768]{4,3,2,1,0:T(8,128)(2,1)}, u32[]{:S(2)}, u32[]{:S(2)}) collective-permute-start(bf16[3,1,2,32,768]{4,3,2,1,0:T(8,128)(2,1)} %get-tuple-element.67), channel_id=1, source_target_pairs={{1,0},{2,1},{3,2},{5,4},{6,5},{7,6},{9,8},{10,9},{11,10},{13,12},{... | collective-permute-start | bytes 884744 | tf_op jit(solution)/shard_map/ppermute | solution.py:19
  28.9 10.1 %collective-permute-start.2 = (bf16[3,1,2,32,768]{4,3,2,1,0:T(8,128)(2,1)}, bf16[3,1,2,32,768]{4,3,2,1,0:T(8,128)(2,1)}, u32[]{:S(2)}, u32[]{:S(2)}) collective-permute-start(bf16[3,1,2,32,768]{4,3,2,1,0:T(8,128)(2,1)} %get-tuple-element.66), channel_id=1, source_target_pairs={{0,1},{1,2},{2,3},{4,5},{5,6},{6,7},{8,9},{9,10},{10,11},{12,13},{... | collective-permute-start | bytes 884744 | tf_op jit(solution)/shard_map/ppermute | solution.py:18
  35.2 2.4 %copy-start.6 = (bf16[768,6,128]{0,2,1:T(8,128)(2,1)}, bf16[768,6,128]{0,2,1:T(8,128)(2,1)S(1)}, u32[]{:S(2)}) copy-start(bf16[768,6,128]{0,2,1:T(8,128)(2,1)S(1)} %copy.29) | copy-start | bytes 3538948
  37.5 1.4 %copy-start.8 = (f32[6,768,128]{2,1,0:T(8,128)}, f32[6,768,128]{2,1,0:T(8,128)S(1)}, u32[]{:S(2)}) copy-start(f32[6,768,128]{2,1,0:T(8,128)S(1)} %get-tuple-element.71) | copy-start | bytes 7077892
  37.6 1.4 %copy-start.19 = (bf16[1,4,32,768]{3,2,1,0:T(8,128)(2,1)S(1)}, bf16[1,4,32,768]{3,2,1,0:T(8,128)(2,1)}, u32[]{:S(2)}) copy-start(bf16[1,4,32,768]{3,2,1,0:T(8,128)(2,1)} %param.15) | copy-start | bytes 589828
  37.6 1.5 %copy-start.21 = (bf16[1,2,2,32,768]{4,3,2,1,0:T(8,128)(2,1)S(1)}, bf16[1,2,2,32,768]{4,3,2,1,0:T(8,128)(2,1)}, u32[]{:S(2)}) copy-start(bf16[1,2,2,32,768]{4,3,2,1,0:T(8,128)(2,1)} %copy-done.20) | copy-start | bytes 589828
  37.6 1.8 %copy-start.23 = (bf16[1,2,2,32,768]{4,3,2,1,0:T(8,128)(2,1)S(1)}, bf16[1,2,2,32,768]{4,3,2,1,0:T(8,128)(2,1)}, u32[]{:S(2)}) copy-start(bf16[1,2,2,32,768]{4,3,2,1,0:T(8,128)(2,1)} %copy-done.22) | copy-start | bytes 589828
  39.4 3.6 %copy-start.9 = (f32[6,768,128]{2,1,0:T(8,128)S(1)}, f32[6,768,128]{2,1,0:T(8,128)}, u32[]{:S(2)}) copy-start(f32[6,768,128]{2,1,0:T(8,128)} %copy-done.8) | copy-start | bytes 7077892
  43.0 5.2 %copy-start.15 = (bf16[128,6,128]{2,1,0:T(8,128)(2,1)S(1)}, bf16[128,6,128]{2,1,0:T(8,128)(2,1)}, u32[]{:S(2)}) copy-start(bf16[128,6,128]{2,1,0:T(8,128)(2,1)} %reshape.347) | copy-start | bytes 589828
  43.0 6.9 %copy-start.12 = (s32[128,768]{0,1:T(8,128)S(1)}, s32[128,768]{0,1:T(8,128)}, u32[]{:S(2)}) copy-start(s32[128,768]{0,1:T(8,128)} %copy-done.11) | copy-start | bytes 1179652
  49.9 4.0 %copy-start.16 = (bf16[128,6,128]{2,1,0:T(8,128)(2,1)S(1)}, bf16[128,6,128]{2,1,0:T(8,128)(2,1)}, u32[]{:S(2)}) copy-start(bf16[128,6,128]{2,1,0:T(8,128)(2,1)} %reshape.345) | copy-start | bytes 589828
  52.8 1.0 copy-start.4
  55.7 9.6 %copy-start.13 = (s32[128,768]{0,1:T(8,128)S(1)}, s32[128,768]{0,1:T(8,128)}, u32[]{:S(2)}) copy-start(s32[128,768]{0,1:T(8,128)} %copy-done.11) | copy-start | bytes 1179652
  57.5 7.9 %copy-start.10 = (f32[6,768,128]{2,1,0:T(8,128)S(1)}, f32[6,768,128]{2,1,0:T(8,128)}, u32[]{:S(2)}) copy-start(f32[6,768,128]{2,1,0:T(8,128)} %copy-done.8) | copy-start | bytes 7077892
  60.0 17.2 %collective-permute-start.8 = (f32[3,2,32,768]{3,2,1,0:T(8,128)}, f32[3,2,32,768]{3,2,1,0:T(8,128)}, u32[]{:S(2)}, u32[]{:S(2)}) collective-permute-start(f32[3,2,32,768]{3,2,1,0:T(8,128)} %get-tuple-element.59), channel_id=1, source_target_pairs={{0,1},{1,2},{2,3},{4,5},{5,6},{6,7},{8,9},{9,10},{10,11},{12,13},{... | collective-permute-start | bytes 1769480 | tf_op jit(solution)/shard_map/ppermute | solution.py:27
  62.0 16.6 %collective-permute-start.9 = (f32[3,2,32,768]{3,2,1,0:T(8,128)}, f32[3,2,32,768]{3,2,1,0:T(8,128)}, u32[]{:S(2)}, u32[]{:S(2)}) collective-permute-start(f32[3,2,32,768]{3,2,1,0:T(8,128)} %get-tuple-element.58), channel_id=1, source_target_pairs={{1,0},{2,1},{3,2},{5,4},{6,5},{7,6},{9,8},{10,9},{11,10},{13,12},{... | collective-permute-start | bytes 1769480 | tf_op jit(solution)/shard_map/ppermute | solution.py:27
  70.8 1.7 %copy-start = (f32[3,8,32,768]{3,2,1,0:T(8,128)S(1)}, f32[3,8,32,768]{3,2,1,0:T(8,128)}, u32[]{:S(2)}) copy-start(f32[3,8,32,768]{3,2,1,0:T(8,128)} %reshape.350) | copy-start | bytes 7077892
  70.8 6.4 %slice-start.1 = ((f32[3,8,32,768]{3,2,1,0:T(8,128)}), f32[3,4,32,768]{3,2,1,0:T(8,128)S(1)}, s32[]{:S(2)}) async-start(f32[3,8,32,768]{3,2,1,0:T(8,128)} %reshape.349), calls=%async_computation.1 | async-start | bytes 2359296 | tf_op jit(solution)/shard_map/slice | solution.py:124
  72.5 14.6 %collective-permute-start.12 = (f32[3,2,32,768]{3,2,1,0:T(8,128)S(1)}, f32[3,2,32,768]{3,2,1,0:T(8,128)S(1)}, u32[]{:S(2)}, u32[]{:S(2)}) collective-permute-start(f32[3,2,32,768]{3,2,1,0:T(8,128)S(1)} %get-tuple-element.57), channel_id=1, source_target_pairs={{0,1},{1,2},{2,3},{4,5},{5,6},{6,7},{8,9},{9,10},{10,11},{12,13},{... | collective-permute-start | bytes 1769480 | tf_op jit(solution)/shard_map/ppermute | solution.py:27
  74.9 12.3 %copy-start.1 = (f32[3,8,32,768]{3,2,1,0:T(8,128)S(1)}, f32[3,8,32,768]{3,2,1,0:T(8,128)}, u32[]{:S(2)}) copy-start(f32[3,8,32,768]{3,2,1,0:T(8,128)} %reshape.350) | copy-start | bytes 7077892
  74.9 12.3 %slice-start = ((f32[3,8,32,768]{3,2,1,0:T(8,128)}), f32[3,4,32,768]{3,2,1,0:T(8,128)S(1)}, s32[]{:S(2)}) async-start(f32[3,8,32,768]{3,2,1,0:T(8,128)} %reshape.350), calls=%async_computation | async-start | bytes 2359296 | tf_op jit(solution)/shard_map/slice | solution.py:125
  74.9 12.3 %collective-permute-start.13 = (f32[3,2,32,768]{3,2,1,0:T(8,128)S(1)}, f32[3,2,32,768]{3,2,1,0:T(8,128)S(1)}, u32[]{:S(2)}, u32[]{:S(2)}) collective-permute-start(f32[3,2,32,768]{3,2,1,0:T(8,128)S(1)} %get-tuple-element.56), channel_id=1, source_target_pairs={{1,0},{2,1},{3,2},{5,4},{6,5},{7,6},{9,8},{10,9},{11,10},{13,12},{... | collective-permute-start | bytes 1769480 | tf_op jit(solution)/shard_map/ppermute | solution.py:27
  79.8 7.7 %copy-start.2 = (f32[3,4,32,768]{3,2,1,0:T(8,128)}, f32[3,4,32,768]{3,2,1,0:T(8,128)S(1)}, u32[]{:S(2)}) copy-start(f32[3,4,32,768]{3,2,1,0:T(8,128)S(1)} %fusion.9) | copy-start | bytes 3538948
  80.8 16.6 %collective-permute-start.11 = (f32[1,4,32,768]{3,2,1,0:T(8,128)}, f32[1,4,32,768]{3,2,1,0:T(8,128)}, u32[]{:S(2)}, u32[]{:S(2)}) collective-permute-start(f32[1,4,32,768]{3,2,1,0:T(8,128)} %get-tuple-element.63), channel_id=1, source_target_pairs={{4,0},{8,4},{12,8},{16,12},{20,16},{24,20},{28,24},{5,1},{9,5},{13... | collective-permute-start | bytes 1179656 | tf_op jit(solution)/shard_map/ppermute | solution.py:27
  82.7 12.0 %copy-start.5 = (bf16[6,128,768]{1,2,0:T(8,128)(2,1)S(1)}, bf16[6,128,768]{1,2,0:T(8,128)(2,1)}, u32[]{:S(2)}) copy-start(bf16[6,128,768]{1,2,0:T(8,128)(2,1)} %copy-done.4) | copy-start | bytes 3538948
  82.7 12.0 %copy-start.7 = (bf16[768,6,128]{0,2,1:T(8,128)(2,1)S(1)}, bf16[768,6,128]{0,2,1:T(8,128)(2,1)}, u32[]{:S(2)}) copy-start(bf16[768,6,128]{0,2,1:T(8,128)(2,1)} %copy-done.6) | copy-start | bytes 3538948
  82.8 29.0 %collective-permute-start.10 = (f32[1,4,32,768]{3,2,1,0:T(8,128)}, f32[1,4,32,768]{3,2,1,0:T(8,128)}, u32[]{:S(2)}, u32[]{:S(2)}) collective-permute-start(f32[1,4,32,768]{3,2,1,0:T(8,128)} %get-tuple-element.62), channel_id=1, source_target_pairs={{0,4},{4,8},{8,12},{12,16},{16,20},{20,24},{24,28},{1,5},{5,9},{9,... | collective-permute-start | bytes 1179656 | tf_op jit(solution)/shard_map/ppermute | solution.py:27
  87.4 7.8 %copy-start.24 = (bf16[6,128,128]{2,1,0:T(8,128)(2,1)S(1)}, bf16[6,128,128]{2,1,0:T(8,128)(2,1)}, u32[]{:S(2)}) copy-start(bf16[6,128,128]{2,1,0:T(8,128)(2,1)} %get-tuple-element.73) | copy-start | bytes 589828
  88.4 23.3 %copy-start.3 = (f32[3,4,32,768]{3,2,1,0:T(8,128)S(1)}, f32[3,4,32,768]{3,2,1,0:T(8,128)}, u32[]{:S(2)}) copy-start(f32[3,4,32,768]{3,2,1,0:T(8,128)} %copy-done.2) | copy-start | bytes 3538948
  88.4 25.2 %collective-permute-start.15 = (f32[1,4,32,768]{3,2,1,0:T(8,128)}, f32[1,4,32,768]{3,2,1,0:T(8,128)S(1)}, u32[]{:S(2)}, u32[]{:S(2)}) collective-permute-start(f32[1,4,32,768]{3,2,1,0:T(8,128)} %get-tuple-element.61), channel_id=1, source_target_pairs={{4,0},{8,4},{12,8},{16,12},{20,16},{24,20},{28,24},{5,1},{9,5},{13... | collective-permute-start | bytes 1179656 | tf_op jit(solution)/shard_map/ppermute | solution.py:27
  90.5 29.7 %collective-permute-start.14 = (f32[1,4,32,768]{3,2,1,0:T(8,128)}, f32[1,4,32,768]{3,2,1,0:T(8,128)}, u32[]{:S(2)}, u32[]{:S(2)}) collective-permute-start(f32[1,4,32,768]{3,2,1,0:T(8,128)} %get-tuple-element.60), channel_id=1, source_target_pairs={{0,4},{4,8},{8,12},{12,16},{16,20},{20,24},{24,28},{1,5},{5,9},{9,... | collective-permute-start | bytes 1179656 | tf_op jit(solution)/shard_map/ppermute | solution.py:27
where the time goes:
time: 123 us; the launch traced here: 122 us
  starting transfers between devices  46.5 us (38%)
  local copies, waits for them, and re-layouts  28.7 us (23%)
  waiting for transfers between devices  21.7 us (18%)
  matrix products  12.4 us (10%)
  other arithmetic  11.2 us (9%)
  between operations  1.32 us (1%)
    ppermute x8, starting transfers between devices, from_behind(): return lax.ppermute(x, axis, pairs)  22.5 us
    ppermute x8, waiting for transfers between devices, from_behind(): return lax.ppermute(x, axis, pairs)  20.9 us
    ppermute x4, starting transfers between devices, padded(): before = lax.ppermute(last, axis, up)  15.2 us
    ppermute x4, starting transfers between devices, padded(): after = lax.ppermute(leading, axis, down)  8.79 us
    reshape x5, local copies, waits for them, and re-layouts, by_head(): return array.reshape(-1, head_count, head_size)  8.37 us
    unnamed x51, local copies, waits for them, and re-layouts  4.56 us
    dot_general x1, matrix products, on_device(): jnp.einsum('hqk,khd->qhd', weights_low, near_values, preferred_element_ty...  3.91 us
    dot_general x1, matrix products, on_device(): jnp.einsum('qhd,khd->hqk', local_grad, near_values, preferred_element_typ...  2.96 us
  transfers between devices with their start and end apart: 16, of which 3 were waited for; matrix products, arithmetic and copies ran while one was open for 23% of the time, Pallas kernels for 0%

commit v1 on v0

v1 whole, which is shorter than its diff:
```python
import functools
import math

import jax
import jax.numpy as jnp
from jax import lax
from jax.experimental import pallas as pl
from jax.experimental.pallas import tpu as pltpu
from jax.sharding import PartitionSpec as P

masked_score = -1e30
MESH = pl.DeviceIdType.MESH
ORDER = (1, 2, 0, 3)


def dot_nt(a, b):
    return lax.dot_general(a, b, (((1,), (1,)), ((), ())), preferred_element_type=jnp.float32)


def dot_nn(a, b):
    return lax.dot_general(a, b, (((1,), (0,)), ((), ())), preferred_element_type=jnp.float32)


def kernel(
    sizes,
    win_ref,
    q_ref,
    k_ref,
    v_ref,
    g_ref,
    att_ref,
    gq_ref,
    gk_ref,
    gv_ref,
    near,
    stat_cols,
    st_main,
    st_down,
    st_up,
    load_sem,
    send_sem,
    recv_sem,
    stat_send,
    stat_recv,
):
    head_count, head_size, row_count, col_count, n_tm, n_space, chunks = sizes
    tokens = row_count * col_count
    half = tokens // 2
    width = head_count * head_size // chunks
    heads_in = width // head_size
    scale = 1.0 / math.sqrt(head_size)
    inputs = (q_ref, k_ref, v_ref, g_ref)
    tm, sp = lax.axis_index("tm"), lax.axis_index("space")
    side = lax.rem(tm, 2)
    pair = tm + 1 - 2 * side
    other = tm - 1 + 2 * side
    relay_to = tm + 2 - 4 * side
    relay_from = tm - 2 + 4 * side
    has_other = (other >= 0) & (other < n_tm)
    has_to = (relay_to >= 0) & (relay_to < n_tm)
    has_from = (relay_from >= 0) & (relay_from < n_tm)
    has_up = sp > 0
    has_down = sp < n_space - 1

    st_main[...] = jnp.zeros_like(st_main)
    st_down[...] = jnp.zeros_like(st_down)
    st_up[...] = jnp.zeros_like(st_up)

    barrier = pltpu.get_barrier_semaphore()

    def greet(cond, tm_to, sp_to):
        @pl.when(cond)
        def _():
            pl.semaphore_signal(barrier, inc=1, device_id=(tm_to, sp_to), device_id_type=MESH)

    pl.semaphore_signal(barrier, inc=1, device_id=(pair, sp), device_id_type=MESH)
    greet(has_to, relay_to, sp)
    greet(has_from, relay_from, sp)
    greet(has_up, tm, sp - 1)
    greet(has_down, tm, sp + 1)

    pieces = [(a, c) for group in ((1, 2), (0, 3)) for c in range(chunks) for a in group]

    def load(j):
        a, c = pieces[j]
        return pltpu.make_async_copy(
            inputs[a].at[:, c * width : (c + 1) * width],
            near.at[a, c, 0, 0:tokens, :],
            load_sem.at[j],
        )

    def remote(src, dst, j, i, device):
        return pltpu.make_async_remote_copy(
            src_ref=src,
            dst_ref=dst,
            send_sem=send_sem.at[j, i],
            recv_sem=recv_sem.at[j, i],
            device_id=device,
            device_id_type=MESH,
        )

    def to_pair(j):
        a, c = pieces[j]
        return remote(
            inputs[a].at[:, c * width : (c + 1) * width],
            near.at[a, c, 1, 0:tokens, :],
            j,
            0,
            (pair, sp),
        )

    def to_relay(j):
        a, c = pieces[j]
        return remote(
            near.at[a, c, 1, 0:tokens, :], near.at[a, c, 2, 0:tokens, :], j, 1, (relay_to, sp)
        )

    def to_up(j, slot):
        a, c = pieces[j]
        if slot == 0:
            src = inputs[a].at[0:half, c * width : (c + 1) * width]
        else:
            src = near.at[a, c, slot, 0:half, :]
        dst = near.at[a, c, slot, tokens : tokens + half, :]
        return remote(src, dst, j, 2 + slot, (tm, sp - 1))

    def to_down(j, slot):
        a, c = pieces[j]
        if slot == 0:
            src = inputs[a].at[half:tokens, c * width : (c + 1) * width]
        else:
            src = near.at[a, c, slot, half:tokens, :]
        dst = near.at[a, c, slot, tokens + half : 2 * tokens, :]
        return remote(src, dst, j, 5 + slot, (tm, sp + 1))

    def rows_out(j, slot):
        @pl.when(has_up)
        def _():
            to_up(j, slot).start()

        @pl.when(has_down)
        def _():
            to_down(j, slot).start()

    def pass_on(j):
        rows_out(j, 0)
        to_pair(j).wait_recv()

        @pl.when(has_to)
        def _():
            to_relay(j).start()

        rows_out(j, 1)

    def pass_other(j):
        @pl.when(has_other)
        def _():
            to_relay(j).wait_recv()
            rows_out(j, 2)

    def arrive(j):
        load(j).wait()

        @pl.when(has_down)
        def _():
            to_up(j, 0).wait_recv()
            to_up(j, 1).wait_recv()

        @pl.when(has_up)
        def _():
            to_down(j, 0).wait_recv()
            to_down(j, 1).wait_recv()

        @pl.when(has_down & has_other)
        def _():
            to_up(j, 2).wait_recv()

        @pl.when(has_up & has_other)
        def _():
            to_down(j, 2).wait_recv()

    count = len(pieces)
    for j in range(count):
        load(j).start()

    expected = (
        1
        + has_to.astype(jnp.int32)
        + has_from.astype(jnp.int32)
        + has_up.astype(jnp.int32)
        + has_down.astype(jnp.int32)
    )
    pl.semaphore_wait(barrier, expected)
    for j in range(count):
        to_pair(j).start()

    @pl.when(jnp.logical_not(has_other))
    def _():
        for a in range(4):
            for c in range(chunks):
                near[a, c, 2] = jnp.zeros((2 * tokens, width), near.dtype)

    @pl.when(jnp.logical_not(has_down))
    def _():
        for a in range(4):
            for c in range(chunks):
                near[a, c, :, tokens : tokens + half, :] = jnp.zeros((3, half, width), near.dtype)

    @pl.when(jnp.logical_not(has_up))
    def _():
        for a in range(4):
            for c in range(chunks):
                near[a, c, :, tokens + half : 2 * tokens, :] = jnp.zeros(
                    (3, half, width), near.dtype
                )

    own_id = lax.broadcasted_iota(jnp.int32, (tokens, 2 * tokens), 0)
    near_id = lax.broadcasted_iota(jnp.int32, (tokens, 2 * tokens), 1)
    own_row, own_col = own_id // col_count, own_id % col_count
    near_row, near_col = near_id // col_count, near_id % col_count
    upper = near_row >= row_count + row_count // 2
    near_row = jnp.where(upper, near_row - 2 * row_count, near_row)
    global_row = sp * row_count + near_row
    row_inside = (global_row >= 0) & (global_row < n_space * row_count)
    row_gap = jnp.where(row_inside, jnp.abs(own_row - near_row), 1 << 20)
    col_gap = jnp.abs(own_col - near_col)
    other_gap = jnp.where(has_other, 0, 1 << 20)

    def window(h):
        col_in = col_gap <= win_ref[1, h]
        here = (row_gap <= win_ref[0, h]) & col_in
        there = (row_gap + other_gap <= win_ref[0, h]) & col_in
        return jnp.concatenate([here, here, there], axis=1)

    lane = lax.broadcasted_iota(jnp.int32, (tokens, tokens), 1)

    def forward(c):
        for e in range(heads_in):
            h = c * heads_in + e
            cols = slice(e * head_size, (e + 1) * head_size)
            out_cols = slice(h * head_size, (h + 1) * head_size)
            query = near[0, c, 0, 0:tokens, cols]
            grad = near[3, c, 0, 0:tokens, cols]
            keys = near[1, c, :, :, cols].reshape(6 * tokens, head_size)
            vals = near[2, c, :, :, cols].reshape(6 * tokens, head_size)
            scores = jnp.where(window(h), dot_nt(query, keys) * scale, masked_score)
            top = jnp.max(scores, axis=1, keepdims=True)
            powers = jnp.exp(scores - top)
            total = jnp.sum(powers, axis=1, keepdims=True)
            soft = powers * (1.0 / total)
            attended = dot_nn(soft.astype(jnp.bfloat16), vals).astype(jnp.bfloat16)
            att_ref[:, out_cols] = attended
            out_dot = jnp.sum(
                grad.astype(jnp.float32) * attended.astype(jnp.float32), axis=1, keepdims=True
            )
            grad_scores = (soft * (dot_nt(grad, vals) - out_dot)).astype(jnp.bfloat16)
            gq_ref[:, out_cols] = (dot_nn(grad_scores, keys) * scale).astype(jnp.bfloat16)
            log_total = top + jnp.log(total)
            stats = jnp.where(lane == h, log_total, stat_cols[...])
            stat_cols[...] = jnp.where(lane == 8 + h, out_dot, stats)

    row_lane = lax.broadcasted_iota(jnp.int32, (1, tokens), 1)

    def stat_row(r):
        parts = []
        for slot in range(3):
            parts.append(st_main[slot, r : r + 1, :])
            parts.append(
                jnp.where(row_lane < half, st_down[slot, r : r + 1, :], st_up[slot, r : r + 1, :])
            )
        return jnp.concatenate(parts, axis=1)

    def backward(c):
        for e in range(heads_in):
            h = c * heads_in + e
            cols = slice(e * head_size, (e + 1) * head_size)
            out_cols = slice(h * head_size, (h + 1) * head_size)
            key = near[1, c, 0, 0:tokens, cols]
            val = near[2, c, 0, 0:tokens, cols]
            queries = near[0, c, :, :, cols].reshape(6 * tokens, head_size)
            grads = near[3, c, :, :, cols].reshape(6 * tokens, head_size)
            scores = dot_nt(key, queries) * scale - stat_row(h)
            soft = jnp.exp(jnp.where(window(h), scores, masked_score))
            gv_ref[:, out_cols] = dot_nn(soft.astype(jnp.bfloat16), grads).astype(jnp.bfloat16)
            grad_scores = (soft * (dot_nt(val, grads) - stat_row(8 + h))).astype(jnp.bfloat16)
            gk_ref[:, out_cols] = (dot_nn(grad_scores, queries) * scale).astype(jnp.bfloat16)

    def stat_copies():
        targets = [
            (None, st_main.at[1], (pair, sp)),
            (has_other, st_main.at[2], (other, sp)),
        ]
        for slot, (cond, frame) in enumerate(((None, tm), (None, pair), (has_other, other))):
            for at, there, cond_s in ((st_down, sp - 1, has_up), (st_up, sp + 1, has_down)):
                both = cond_s if cond is None else cond & cond_s
                targets.append((both, at.at[slot], (frame, there)))
        arrivals = [None, has_other]
        for cond in (None, None, has_other):
            for cond_s in (has_down, has_up):
                arrivals.append(cond_s if cond is None else cond & cond_s)
        found = []
        for i, (cond, dst, device) in enumerate(targets):
            copy = pltpu.make_async_remote_copy(
                src_ref=st_main.at[0],
                dst_ref=dst,
                send_sem=stat_send.at[i],
                recv_sem=stat_recv.at[i],
                device_id=device,
                device_id_type=MESH,
            )
            found.append((cond, arrivals[i], copy))
        return found

    def when(cond, action):
        if cond is None:
            action()
        else:
            pl.when(cond)(action)

    stat_cols[...] = jnp.zeros_like(stat_cols)
    per = 2
    lag = 1

    def own_ready(c):
        load(per * chunks + per * c).wait()
        load(per * chunks + per * c + 1).wait()

    def arrive_halo(j):
        @pl.when(has_down)
        def _():
            to_up(j, 0).wait_recv()
            to_up(j, 1).wait_recv()

        @pl.when(has_up)
        def _():
            to_down(j, 0).wait_recv()
            to_down(j, 1).wait_recv()

        @pl.when(has_down & has_other)
        def _():
            to_up(j, 2).wait_recv()

        @pl.when(has_up & has_other)
        def _():
            to_down(j, 2).wait_recv()

    def compute_forward(c):
        own_ready(c)
        for j in (per * c, per * c + 1):
            load(j).wait()
            arrive_halo(j)
        forward(c)

    def compute_backward(c):
        for j in (per * (chunks + c), per * (chunks + c) + 1):
            arrive_halo(j)
        backward(c)

    done_f = 0
    done_b = 0
    for j in range(count + lag):
        if j < count:
            pass_on(j)
        if j >= lag:
            pass_other(j - lag)
        if done_f < chunks and j >= per * (done_f + 1) + lag:
            compute_forward(done_f)
            done_f += 1
            if done_f == chunks:
                st_main[0] = stat_cols[...].T[0:16, :]
                for cond, _, copy in stat_copies():
                    when(cond, copy.start)
    for _, cond, copy in stat_copies():
        when(cond, copy.wait_recv)
    for c in range(chunks):
        compute_backward(c)

    for cond, _, copy in stat_copies():
        when(cond, copy.wait_send)
    for j in range(count):
        to_pair(j).wait_send()
        when(has_to, to_relay(j).wait_send)
        for slot in range(3):
            extra = has_other if slot == 2 else None
            when(has_up if extra is None else has_up & extra, to_up(j, slot).wait_send)
            when(has_down if extra is None else has_down & extra, to_down(j, slot).wait_send)


def on_device(queries, key_vectors, values, grad_out, windows):
    local_shape = queries.shape
    row_count, col_count, features = local_shape[1:]
    head_count = windows.shape[1]
    head_size = features // head_count
    tokens = row_count * col_count
    chunks = head_count // 2 if head_count % 2 == 0 else head_count
    width = features // chunks
    sizes = (
        head_count,
        head_size,
        row_count,
        col_count,
        lax.axis_size("tm"),
        lax.axis_size("space"),
        chunks,
    )
    flat = (tokens, features)
    count = 4 * chunks
    outs = pl.pallas_call(
        functools.partial(kernel, sizes),
        out_shape=[jax.ShapeDtypeStruct(flat, jnp.bfloat16)] * 4,
        in_specs=[pl.BlockSpec(memory_space=pltpu.SMEM)]
        + [pl.BlockSpec(memory_space=pl.ANY)] * 4,
        out_specs=[pl.BlockSpec(memory_space=pltpu.VMEM)] * 4,
        scratch_shapes=[
            pltpu.VMEM((4, chunks, 3, 2 * tokens, width), jnp.bfloat16),
            pltpu.VMEM((tokens, tokens), jnp.float32),
            pltpu.VMEM((3, 16, tokens), jnp.float32),
            pltpu.VMEM((3, 16, tokens), jnp.float32),
            pltpu.VMEM((3, 16, tokens), jnp.float32),
            pltpu.SemaphoreType.DMA((count,)),
            pltpu.SemaphoreType.DMA((count, 8)),
            pltpu.SemaphoreType.DMA((count, 8)),
            pltpu.SemaphoreType.DMA((8,)),
            pltpu.SemaphoreType.DMA((8,)),
        ],
        compiler_params=pltpu.CompilerParams(
            collective_id=0, has_side_effects=True, vmem_limit_bytes=40 * 1024 * 1024
        ),
    )(
        windows,
        queries.reshape(flat),
        key_vectors.reshape(flat),
        values.reshape(flat),
        grad_out.reshape(flat),
    )
    return tuple(out.reshape(local_shape) for out in outs)


def solution(mesh):
    spec = P("tm", "space", None, None)
    return jax.shard_map(
        on_device,
        mesh=mesh,
        in_specs=(spec, spec, spec, spec, P()),
        out_specs=(spec, spec, spec, spec),
        check_vma=False,
    )
```

time: 123 us -> 47.6 us (0.39)
  starting transfers between devices: 46.5 us -> 0 us
  Pallas kernels: 0 us -> 39.6 us
  waiting for transfers between devices: 21.7 us -> 0 us
  local copies, waits for them, and re-layouts: 28.7 us -> 7.09 us
  matrix products: 12.4 us -> 0 us
  other arithmetic: 11.2 us -> 0 us
    ppermute x16 -> x0, starting transfers between devices: 46.5 us -> none  [the longest x8 22.5 us: from_behind(): return lax.ppermute(x, axis, pairs)]
    pallas_call x0 -> x1, Pallas kernels: none -> 39.6 us  [on_device(): pl.pallas_call(functools.partial(kernel, sizes), out_shape=[jax.ShapeDtyp...]
    ppermute x16 -> x0, waiting for transfers between devices: 21.7 us -> none  [the longest x8 20.9 us: from_behind(): return lax.ppermute(x, axis, pairs)]
    reshape x9 -> x0, local copies, waits for them, and re-layouts: 13.7 us -> none  [the longest x5 8.37 us: by_head(): return array.reshape(-1, head_count, head_size)]
    dot_general x6 -> x0, matrix products: 12.4 us -> none  [the longest x1 3.91 us: on_device(): jnp.einsum('hqk,khd->qhd', weights_low, near_values, preferred_element_ty...]
    slice x10 -> x0, local copies, waits for them, and re-layouts: 5.56 us -> none  [the longest x1 2.54 us: on_device(): part_keys[:, rim_start:rim_start + row_extent]]
    convert_element_type x2 -> x0, other arithmetic: 3.58 us -> none  [the longest x1 1.85 us: on_device(): grad_keys = own_keys.astype(jnp.bfloat16)]
    scatter-add x4 -> x0, other arithmetic: 2.73 us -> none  [the longest x2 2.52 us: on_device(): centre_keys = centre_keys.at[:, land_at:land_at + row_extent].add(got_keys)]
  transfers between devices with their start and end apart: 16 -> 0, of which waited for: 3 -> 0; matrix products, arithmetic and copies ran while one was open for 23% -> 0% of each run, Pallas kernels for 0% -> 0%
where the time goes in v1:
time: 47.6 us; the launch traced here: 47.3 us
  Pallas kernels  39.6 us (83%)
  local copies, waits for them, and re-layouts  7.09 us (15%)
  between operations  0.65 us (1%)
    pallas_call x1, Pallas kernels, on_device(): pl.pallas_call(functools.partial(kernel, sizes), out_shape=[jax.ShapeDtyp...  39.6 us
    unnamed x14, local copies, waits for them, and re-layouts  7.09 us

profile of v1, /device:TPU:5, one launch (start us, length us, event | category | flops | bytes accessed | tf_op | source)
XLA Modules:
  0.0 47.3 jit_solution(17018424120603060740)
XLA Ops:
  0.6 0.0 copy-start.4
  0.6 0.7 %copy-done.4 = s32[2,6]{1,0:T(2,128)S(1)} copy-done((s32[2,6]{1,0:T(2,128)S(1)}, s32[2,6]{1,0:T(2,128)}, u32[]{:S(2)}) %copy-start.4) | copy-done | bytes 72
  1.3 0.0 copy-start
  1.3 0.9 %copy-done = bf16[1,4,32,768]{3,2,1,0:T(8,128)(2,1)S(1)} copy-done((bf16[1,4,32,768]{3,2,1,0:T(8,128)(2,1)S(1)}, bf16[1,4,32,768]{3,2,1,0:T(8,128)(2,1)}, u32[]{:S(2)}) %copy-start) | copy-done | bytes 196632
  2.2 0.0 copy-start.1
  2.2 0.9 %copy-done.1 = bf16[1,4,32,768]{3,2,1,0:T(8,128)(2,1)S(1)} copy-done((bf16[1,4,32,768]{3,2,1,0:T(8,128)(2,1)S(1)}, bf16[1,4,32,768]{3,2,1,0:T(8,128)(2,1)}, u32[]{:S(2)}) %copy-start.1) | copy-done | bytes 196632
  3.2 0.0 copy-start.2
  3.2 0.9 %copy-done.2 = bf16[1,4,32,768]{3,2,1,0:T(8,128)(2,1)S(1)} copy-done((bf16[1,4,32,768]{3,2,1,0:T(8,128)(2,1)S(1)}, bf16[1,4,32,768]{3,2,1,0:T(8,128)(2,1)}, u32[]{:S(2)}) %copy-start.2) | copy-done | bytes 196632
  4.1 0.0 copy-start.3
  4.1 0.9 %copy-done.3 = bf16[1,4,32,768]{3,2,1,0:T(8,128)(2,1)S(1)} copy-done((bf16[1,4,32,768]{3,2,1,0:T(8,128)(2,1)S(1)}, bf16[1,4,32,768]{3,2,1,0:T(8,128)(2,1)}, u32[]{:S(2)}) %copy-start.3) | copy-done | bytes 196632
  5.0 39.6 %shard_map.84 = (bf16[128,768]{1,0:T(8,128)(2,1)S(1)}, bf16[128,768]{1,0:T(8,128)(2,1)S(1)}, bf16[128,768]{1,0:T(8,128)(2,1)S(1)}, bf16[128,768]{1,0:T(8,128)(2,1)S(1)}) custom-call(s32[2,6]{1,0:T(2,128)S(1)} %copy-done.4, bf16[128,768]{1,0:T(8,128)(2,1)S(1)} %bitcast.12, bf16[128,768]{1,0:T(8,128)(2,1)S(1)} %bitcast.13, bf16[128,768]{1,0:T(8,128)(2,1)S(1)} %bitcast.14, ...), custom_call_target="tpu_custom_call" | custom-call | tf_op jit(solution)/shard_map/pallas_call | solution.py:408
  44.6 0.7 %copy.13 = bf16[1,4,32,768]{3,2,1,0:T(8,128)(2,1)} copy(bf16[1,4,32,768]{3,2,1,0:T(8,128)(2,1)S(1)} %bitcast.11) | data formatting | bytes 393216
  45.3 0.7 %copy.14 = bf16[1,4,32,768]{3,2,1,0:T(8,128)(2,1)} copy(bf16[1,4,32,768]{3,2,1,0:T(8,128)(2,1)S(1)} %bitcast.10) | data formatting | bytes 393216
  46.0 0.7 %copy.15 = bf16[1,4,32,768]{3,2,1,0:T(8,128)(2,1)} copy(bf16[1,4,32,768]{3,2,1,0:T(8,128)(2,1)S(1)} %bitcast.9) | data formatting | bytes 393216
  46.7 0.7 %copy.16 = bf16[1,4,32,768]{3,2,1,0:T(8,128)(2,1)} copy(bf16[1,4,32,768]{3,2,1,0:T(8,128)(2,1)S(1)} %bitcast.8) | data formatting | bytes 393216
Async XLA Ops:
  0.6 0.7 %copy-start.4 = (s32[2,6]{1,0:T(2,128)S(1)}, s32[2,6]{1,0:T(2,128)}, u32[]{:S(2)}) copy-start(s32[2,6]{1,0:T(2,128)} %win_ref.1) | copy-start | bytes 148
  1.3 0.9 %copy-start = (bf16[1,4,32,768]{3,2,1,0:T(8,128)(2,1)S(1)}, bf16[1,4,32,768]{3,2,1,0:T(8,128)(2,1)}, u32[]{:S(2)}) copy-start(bf16[1,4,32,768]{3,2,1,0:T(8,128)(2,1)} %param.5) | copy-start | bytes 589828
  2.2 0.9 %copy-start.1 = (bf16[1,4,32,768]{3,2,1,0:T(8,128)(2,1)S(1)}, bf16[1,4,32,768]{3,2,1,0:T(8,128)(2,1)}, u32[]{:S(2)}) copy-start(bf16[1,4,32,768]{3,2,1,0:T(8,128)(2,1)} %param.6) | copy-start | bytes 589828
  3.2 0.9 %copy-start.2 = (bf16[1,4,32,768]{3,2,1,0:T(8,128)(2,1)S(1)}, bf16[1,4,32,768]{3,2,1,0:T(8,128)(2,1)}, u32[]{:S(2)}) copy-start(bf16[1,4,32,768]{3,2,1,0:T(8,128)(2,1)} %param.7) | copy-start | bytes 589828
  4.1 0.9 %copy-start.3 = (bf16[1,4,32,768]{3,2,1,0:T(8,128)(2,1)S(1)}, bf16[1,4,32,768]{3,2,1,0:T(8,128)(2,1)}, u32[]{:S(2)}) copy-start(bf16[1,4,32,768]{3,2,1,0:T(8,128)(2,1)} %param.8) | copy-start | bytes 589828

commit v2 on v1

--- a/solution.py
+++ b/solution.py
@@ -10,7 +10,6 @@
 
 masked_score = -1e30
 MESH = pl.DeviceIdType.MESH
-ORDER = (1, 2, 0, 3)
 
 
 def dot_nt(a, b):
@@ -23,11 +22,16 @@
 
 def kernel(
     sizes,
-    win_ref,
+    win_hbm,
     q_ref,
     k_ref,
     v_ref,
     g_ref,
+    att_out,
+    gq_out,
+    gk_out,
+    gv_out,
+    win_ref,
     att_ref,
     gq_ref,
     gk_ref,
@@ -42,6 +46,7 @@
     recv_sem,
     stat_send,
     stat_recv,
+    out_sem,
 ):
     head_count, head_size, row_count, col_count, n_tm, n_space, chunks = sizes
     tokens = row_count * col_count
@@ -158,28 +163,9 @@
             to_relay(j).wait_recv()
             rows_out(j, 2)
 
-    def arrive(j):
-        load(j).wait()
-
-        @pl.when(has_down)
-        def _():
-            to_up(j, 0).wait_recv()
-            to_up(j, 1).wait_recv()
-
-        @pl.when(has_up)
-        def _():
-            to_down(j, 0).wait_recv()
-            to_down(j, 1).wait_recv()
-
-        @pl.when(has_down & has_other)
-        def _():
-            to_up(j, 2).wait_recv()
-
-        @pl.when(has_up & has_other)
-        def _():
-            to_down(j, 2).wait_recv()
-
     count = len(pieces)
+    get_windows = pltpu.make_async_copy(win_hbm, win_ref, load_sem.at[count])
+    get_windows.start()
     for j in range(count):
         load(j).start()
 
@@ -344,17 +330,31 @@
         def _():
             to_down(j, 2).wait_recv()
 
+    results = ((att_ref, att_out), (gq_ref, gq_out), (gk_ref, gk_out), (gv_ref, gv_out))
+
+    def put(i, c):
+        cols = slice(c * width, (c + 1) * width)
+        return pltpu.make_async_copy(
+            results[i][0].at[:, cols], results[i][1].at[:, cols], out_sem.at[i, c]
+        )
+
     def compute_forward(c):
+        if c == 0:
+            get_windows.wait()
         own_ready(c)
         for j in (per * c, per * c + 1):
             load(j).wait()
             arrive_halo(j)
         forward(c)
+        put(0, c).start()
+        put(1, c).start()
 
     def compute_backward(c):
         for j in (per * (chunks + c), per * (chunks + c) + 1):
             arrive_halo(j)
         backward(c)
+        put(2, c).start()
+        put(3, c).start()
 
     done_f = 0
     done_b = 0
@@ -384,6 +384,22 @@
             extra = has_other if slot == 2 else None
             when(has_up if extra is None else has_up & extra, to_up(j, slot).wait_send)
             when(has_down if extra is None else has_down & extra, to_down(j, slot).wait_send)
+    for i in range(4):
+        for c in range(chunks):
+            put(i, c).wait()
+
+
+def put_out(*refs):
+    sources, targets, held, come, go = refs[:4], refs[4:8], refs[8], refs[9], refs[10]
+    ins = [pltpu.make_async_copy(sources[i], held.at[i], come.at[i]) for i in range(4)]
+    outs = [pltpu.make_async_copy(held.at[i], targets[i], go.at[i]) for i in range(4)]
+    for copy in ins:
+        copy.start()
+    for i in range(4):
+        ins[i].wait()
+        outs[i].start()
+    for copy in outs:
+        copy.wait()
 
 
 def on_device(queries, key_vectors, values, grad_out, windows):
@@ -408,23 +424,28 @@
     outs = pl.pallas_call(
         functools.partial(kernel, sizes),
         out_shape=[jax.ShapeDtypeStruct(flat, jnp.bfloat16)] * 4,
-        in_specs=[pl.BlockSpec(memory_space=pltpu.SMEM)]
-        + [pl.BlockSpec(memory_space=pl.ANY)] * 4,
-        out_specs=[pl.BlockSpec(memory_space=pltpu.VMEM)] * 4,
+        in_specs=[pl.BlockSpec(memory_space=pl.ANY)] * 5,
+        out_specs=[pl.BlockSpec(memory_space=pl.ANY)] * 4,
         scratch_shapes=[
+            pltpu.SMEM((2, head_count), jnp.int32),
+            pltpu.VMEM(flat, jnp.bfloat16),
+            pltpu.VMEM(flat, jnp.bfloat16),
+            pltpu.VMEM(flat, jnp.bfloat16),
+            pltpu.VMEM(flat, jnp.bfloat16),
             pltpu.VMEM((4, chunks, 3, 2 * tokens, width), jnp.bfloat16),
             pltpu.VMEM((tokens, tokens), jnp.float32),
             pltpu.VMEM((3, 16, tokens), jnp.float32),
             pltpu.VMEM((3, 16, tokens), jnp.float32),
             pltpu.VMEM((3, 16, tokens), jnp.float32),
-            pltpu.SemaphoreType.DMA((count,)),
+            pltpu.SemaphoreType.DMA((count + 1,)),
             pltpu.SemaphoreType.DMA((count, 8)),
             pltpu.SemaphoreType.DMA((count, 8)),
             pltpu.SemaphoreType.DMA((8,)),
             pltpu.SemaphoreType.DMA((8,)),
+            pltpu.SemaphoreType.DMA((4, chunks)),
         ],
         compiler_params=pltpu.CompilerParams(
-            collective_id=0, has_side_effects=True, vmem_limit_bytes=40 * 1024 * 1024
+            collective_id=0, has_side_effects=True, vmem_limit_bytes=63_000_000
         ),
     )(
         windows,
@@ -433,6 +454,18 @@
         values.reshape(flat),
         grad_out.reshape(flat),
     )
+    outs = pl.pallas_call(
+        put_out,
+        out_shape=[jax.ShapeDtypeStruct(flat, jnp.bfloat16)] * 4,
+        in_specs=[pl.BlockSpec(memory_space=pl.ANY)] * 4,
+        out_specs=[pl.BlockSpec(memory_space=pl.ANY)] * 4,
+        scratch_shapes=[
+            pltpu.VMEM((4,) + flat, jnp.bfloat16),
+            pltpu.SemaphoreType.DMA((4,)),
+            pltpu.SemaphoreType.DMA((4,)),
+        ],
+        compiler_params=pltpu.CompilerParams(vmem_limit_bytes=63_000_000),
+    )(*outs)
     return tuple(out.reshape(local_shape) for out in outs)
 
 

time: 47.6 us -> 43.1 us (0.905)
  local copies, waits for them, and re-layouts: 7.09 us -> 0 us
  Pallas kernels: 39.6 us -> 42.3 us
    unnamed x14 -> x0, local copies, waits for them, and re-layouts: 7.09 us -> none
    pallas_call x0 -> x1, Pallas kernels: none -> 1.96 us  [on_device(): pl.pallas_call(put_out, out_shape=[jax.ShapeDtypeStruct(flat, jnp.bfloat1...]
    pallas_call x1, Pallas kernels: 39.6 us -> 40.3 us  [on_device(): pl.pallas_call(functools.partial(kernel, sizes), out_shape=[jax.ShapeDtyp...]
where the time goes in v2:
time: 43.1 us; the launch traced here: 42.9 us
  Pallas kernels  42.3 us (98%)
  between operations  0.64 us (1%)
    pallas_call x1, Pallas kernels, on_device(): pl.pallas_call(functools.partial(kernel, sizes), out_shape=[jax.ShapeDtyp...  40.3 us
    pallas_call x1, Pallas kernels, on_device(): pl.pallas_call(put_out, out_shape=[jax.ShapeDtypeStruct(flat, jnp.bfloat1...  1.96 us

profile of v2, /device:TPU:5, one launch (start us, length us, event | category | flops | bytes accessed | tf_op | source)
XLA Modules:
  0.0 42.9 jit_solution(13337040364516618618)
XLA Ops:
  0.6 40.3 %shard_map.84 = (bf16[128,768]{1,0:T(8,128)(2,1)}, bf16[128,768]{1,0:T(8,128)(2,1)}, bf16[128,768]{1,0:T(8,128)(2,1)}, bf16[128,768]{1,0:T(8,128)(2,1)}) custom-call(s32[2,6]{1,0:T(2,128)} %win_hbm.1, bf16[128,768]{1,0:T(8,128)(2,1)} %bitcast.8, bf16[128,768]{1,0:T(8,128)(2,1)} %bitcast.9, bf16[128,768]{1,0:T(8,128)(2,1)} %bitcast.10, bf16[128,768]{1,0:T(8,128)(2,1)} %bitcast.11), custom_call_target="tpu_custom_call" | custom-call | tf_op jit(solution)/shard_map/pallas_call | solution.py:424
  41.0 2.0 %shard_map.85 = (bf16[128,768]{1,0:T(8,128)(2,1)}, bf16[128,768]{1,0:T(8,128)(2,1)}, bf16[128,768]{1,0:T(8,128)(2,1)}, bf16[128,768]{1,0:T(8,128)(2,1)}) custom-call(bf16[128,768]{1,0:T(8,128)(2,1)} %get-tuple-element.12.refs_0_, bf16[128,768]{1,0:T(8,128)(2,1)} %get-tuple-element.13.refs_1_, bf16[128,768]{1,0:T(8,128)(2,1)} %get-tuple-element.14.refs_2_, ...), custom_call_target="tpu_custom_call" | custom-call | tf_op jit(solution)/shard_map/pallas_call | solution.py:457

commit v3 on v2

v3 whole, which is shorter than its diff:
```python
import functools
import math

import jax
import jax.numpy as jnp
from jax import lax
from jax.experimental import pallas as pl
from jax.experimental.pallas import tpu as pltpu
from jax.sharding import PartitionSpec as P

masked_score = -1e30
MESH = pl.DeviceIdType.MESH


def dot_nt(a, b):
    return lax.dot_general(a, b, (((1,), (1,)), ((), ())), preferred_element_type=jnp.float32)


def dot_nn(a, b):
    return lax.dot_general(a, b, (((1,), (0,)), ((), ())), preferred_element_type=jnp.float32)


def kernel(
    sizes,
    win_hbm,
    q_ref,
    k_ref,
    v_ref,
    g_ref,
    att_out,
    gq_out,
    gk_out,
    gv_out,
    win_ref,
    att_ref,
    gq_ref,
    gk_ref,
    gv_ref,
    near,
    stat_cols,
    st_main,
    st_down,
    st_up,
    load_sem,
    send_sem,
    recv_sem,
    stat_send,
    stat_recv,
    out_sem,
):
    head_count, head_size, row_count, col_count, n_tm, n_space = sizes
    tokens = row_count * col_count
    half = tokens // 2
    scale = 1.0 / math.sqrt(head_size)
    tm, sp = lax.axis_index("tm"), lax.axis_index("space")
    side = lax.rem(tm, 2)
    pair = tm + 1 - 2 * side
    other = tm - 1 + 2 * side
    relay_to = tm + 2 - 4 * side
    relay_from = tm - 2 + 4 * side
    has_other = (other >= 0) & (other < n_tm)
    has_to = (relay_to >= 0) & (relay_to < n_tm)
    has_from = (relay_from >= 0) & (relay_from < n_tm)
    has_up = sp > 0
    has_down = sp < n_space - 1

    st_main[...] = jnp.zeros_like(st_main)
    st_down[...] = jnp.zeros_like(st_down)
    st_up[...] = jnp.zeros_like(st_up)

    barrier = pltpu.get_barrier_semaphore()

    def greet(cond, tm_to, sp_to):
        @pl.when(cond)
        def _():
            pl.semaphore_signal(barrier, inc=1, device_id=(tm_to, sp_to), device_id_type=MESH)

    pl.semaphore_signal(barrier, inc=1, device_id=(pair, sp), device_id_type=MESH)
    greet(has_to, relay_to, sp)
    greet(has_from, relay_from, sp)
    greet(has_up, tm, sp - 1)
    greet(has_down, tm, sp + 1)

    near_arrays = ((k_ref, v_ref), (q_ref, g_ref))
    pieces = [(phase, h) for phase in range(2) for h in range(head_count)]
    count = len(pieces)

    def block(j, slot, start, size):
        phase, h = pieces[j]
        return near.at[phase, h, :, slot, start : start + size, :]

    def source(j, a):
        phase, h = pieces[j]
        return near_arrays[phase][a].at[:, h * head_size : (h + 1) * head_size]

    def load(j, a):
        phase, h = pieces[j]
        return pltpu.make_async_copy(
            source(j, a), near.at[phase, h, a, 0, 0:tokens, :], load_sem.at[j]
        )

    def load_wait(j):
        whole = block(j, 0, 0, tokens)
        pltpu.make_async_copy(whole, whole, load_sem.at[j]).wait()

    def remote(src, dst, send, recv, device):
        return pltpu.make_async_remote_copy(
            src_ref=src,
            dst_ref=dst,
            send_sem=send,
            recv_sem=recv,
            device_id=device,
            device_id_type=MESH,
        )

    def to_pair(j, a):
        phase, h = pieces[j]
        return remote(
            source(j, a),
            near.at[phase, h, a, 1, 0:tokens, :],
            send_sem.at[0],
            recv_sem.at[j, 0],
            (pair, sp),
        )

    def both_pair(j):
        whole = block(j, 1, 0, tokens)
        return remote(whole, whole, send_sem.at[0], recv_sem.at[j, 0], (pair, sp))

    def to_relay(j):
        return remote(
            block(j, 1, 0, tokens),
            block(j, 2, 0, tokens),
            send_sem.at[1],
            recv_sem.at[j, 1],
            (relay_to, sp),
        )

    def to_up(j, slot, size=None):
        slots = slot if size is None else slice(slot, slot + size)
        late = 1 if slot == 2 else 0
        return remote(
            block(j, slots, 0, half),
            block(j, slots, tokens, half),
            send_sem.at[2 + late],
            recv_sem.at[j, 2 + late],
            (tm, sp - 1),
        )

    def to_down(j, slot, size=None):
        slots = slot if size is None else slice(slot, slot + size)
        late = 1 if slot == 2 else 0
        return remote(
            block(j, slots, half, half),
            block(j, slots, tokens + half, half),
            send_sem.at[4 + late],
            recv_sem.at[j, 4 + late],
            (tm, sp + 1),
        )

    def rows_out(j, slot):
        @pl.when(has_up)
        def _():
            to_up(j, slot).start()

        @pl.when(has_down)
        def _():
            to_down(j, slot).start()

    def pass_on(j):
        if pieces[j][0] == 0:
            load_wait(j)
        rows_out(j, 0)
        both_pair(j).wait_recv()

        @pl.when(has_to)
        def _():
            to_relay(j).start()

        rows_out(j, 1)

    def pass_other(j):
        @pl.when(has_other)
        def _():
            to_relay(j).wait_recv()
            rows_out(j, 2)

    def arrive_halo(j):
        @pl.when(has_down)
        def _():
            to_up(j, 0, 2).wait_recv()

        @pl.when(has_up)
        def _():
            to_down(j, 0, 2).wait_recv()

        @pl.when(has_down & has_other)
        def _():
            to_up(j, 2).wait_recv()

        @pl.when(has_up & has_other)
        def _():
            to_down(j, 2).wait_recv()

    get_windows = pltpu.make_async_copy(win_hbm, win_ref, load_sem.at[count])
    get_windows.start()
    for j in range(count):
        for a in range(2):
            load(j, a).start()

    expected = (
        1
        + has_to.astype(jnp.int32)
        + has_from.astype(jnp.int32)
        + has_up.astype(jnp.int32)
        + has_down.astype(jnp.int32)
    )
    pl.semaphore_wait(barrier, expected)
    for j in range(count):
        for a in range(2):
            to_pair(j, a).start()

    @pl.when(jnp.logical_not(has_other))
    def _():
        for phase, h in pieces:
            near[phase, h, :, 2] = jnp.zeros((2, 2 * tokens, head_size), near.dtype)

    @pl.when(jnp.logical_not(has_down))
    def _():
        for phase, h in pieces:
            near[phase, h, :, :, tokens : tokens + half, :] = jnp.zeros(
                (2, 3, half, head_size), near.dtype
            )

    @pl.when(jnp.logical_not(has_up))
    def _():
        for phase, h in pieces:
            near[phase, h, :, :, tokens + half : 2 * tokens, :] = jnp.zeros(
                (2, 3, half, head_size), near.dtype
            )

    own_id = lax.broadcasted_iota(jnp.int32, (tokens, 2 * tokens), 0)
    near_id = lax.broadcasted_iota(jnp.int32, (tokens, 2 * tokens), 1)
    own_row, own_col = own_id // col_count, own_id % col_count
    near_row, near_col = near_id // col_count, near_id % col_count
    upper = near_row >= row_count + row_count // 2
    near_row = jnp.where(upper, near_row - 2 * row_count, near_row)
    global_row = sp * row_count + near_row
    row_inside = (global_row >= 0) & (global_row < n_space * row_count)
    row_gap = jnp.where(row_inside, jnp.abs(own_row - near_row), 1 << 20)
    col_gap = jnp.abs(own_col - near_col)
    other_gap = jnp.where(has_other, 0, 1 << 20)

    def window(h):
        col_in = col_gap <= win_ref[1, h]
        here = (row_gap <= win_ref[0, h]) & col_in
        there = (row_gap + other_gap <= win_ref[0, h]) & col_in
        return jnp.concatenate([here, here, there], axis=1)

    lane = lax.broadcasted_iota(jnp.int32, (tokens, tokens), 1)

    def forward(h):
        out_cols = slice(h * head_size, (h + 1) * head_size)
        query = near[1, h, 0, 0, 0:tokens, :]
        grad = near[1, h, 1, 0, 0:tokens, :]
        keys = near[0, h, 0].reshape(6 * tokens, head_size)
        vals = near[0, h, 1].reshape(6 * tokens, head_size)
        scores = jnp.where(window(h), dot_nt(query, keys) * scale, masked_score)
        top = jnp.max(scores, axis=1, keepdims=True)
        powers = jnp.exp(scores - top)
        total = jnp.sum(powers, axis=1, keepdims=True)
        soft = powers * (1.0 / total)
        attended = dot_nn(soft.astype(jnp.bfloat16), vals).astype(jnp.bfloat16)
        att_ref[:, out_cols] = attended
        out_dot = jnp.sum(
            grad.astype(jnp.float32) * attended.astype(jnp.float32), axis=1, keepdims=True
        )
        grad_scores = (soft * (dot_nt(grad, vals) - out_dot)).astype(jnp.bfloat16)
        gq_ref[:, out_cols] = (dot_nn(grad_scores, keys) * scale).astype(jnp.bfloat16)
        log_total = top + jnp.log(total)
        stats = jnp.where(lane == h, log_total, stat_cols[...])
        stat_cols[...] = jnp.where(lane == 8 + h, out_dot, stats)

    row_lane = lax.broadcasted_iota(jnp.int32, (1, tokens), 1)

    def stat_row(r):
        parts = []
        for slot in range(3):
            parts.append(st_main[slot, r : r + 1, :])
            parts.append(
                jnp.where(row_lane < half, st_down[slot, r : r + 1, :], st_up[slot, r : r + 1, :])
            )
        return jnp.concatenate(parts, axis=1)

    def backward(h):
        out_cols = slice(h * head_size, (h + 1) * head_size)
        key = near[0, h, 0, 0, 0:tokens, :]
        val = near[0, h, 1, 0, 0:tokens, :]
        queries = near[1, h, 0].reshape(6 * tokens, head_size)
        grads = near[1, h, 1].reshape(6 * tokens, head_size)
        scores = dot_nt(key, queries) * scale - stat_row(h)
        soft = jnp.exp(jnp.where(window(h), scores, masked_score))
        gv_ref[:, out_cols] = dot_nn(soft.astype(jnp.bfloat16), grads).astype(jnp.bfloat16)
        grad_scores = (soft * (dot_nt(val, grads) - stat_row(8 + h))).astype(jnp.bfloat16)
        gk_ref[:, out_cols] = (dot_nn(grad_scores, queries) * scale).astype(jnp.bfloat16)

    def stat_copies():
        targets = [
            (None, st_main.at[1], (pair, sp)),
            (has_other, st_main.at[2], (other, sp)),
        ]
        for slot, (cond, frame) in enumerate(((None, tm), (None, pair), (has_other, other))):
            for at, there, cond_s in ((st_down, sp - 1, has_up), (st_up, sp + 1, has_down)):
                both = cond_s if cond is None else cond & cond_s
                targets.append((both, at.at[slot], (frame, there)))
        arrivals = [None, has_other]
        for cond in (None, None, has_other):
            for cond_s in (has_down, has_up):
                arrivals.append(cond_s if cond is None else cond & cond_s)
        found = []
        for i, (cond, dst, device) in enumerate(targets):
            copy = pltpu.make_async_remote_copy(
                src_ref=st_main.at[0],
                dst_ref=dst,
                send_sem=stat_send.at[i],
                recv_sem=stat_recv.at[i],
                device_id=device,
                device_id_type=MESH,
            )
            found.append((cond, arrivals[i], copy))
        return found

    def when(cond, action):
        if cond is None:
            action()
        else:
            pl.when(cond)(action)

    stat_cols[...] = jnp.zeros_like(stat_cols)
    lag = 3
    slack = 2
    results = ((att_ref, att_out), (gq_ref, gq_out), (gk_ref, gk_out), (gv_ref, gv_out))

    def put(i, h):
        cols = slice(h * head_size, (h + 1) * head_size)
        return pltpu.make_async_copy(
            results[i][0].at[:, cols], results[i][1].at[:, cols], out_sem.at[i]
        )

    for h in range(head_count):
        load_wait(head_count + h)

    done = 0
    for j in range(count + lag):
        if j < count:
            pass_on(j)
        if j >= lag:
            pass_other(j - lag)
        if done < head_count and j >= min(done + lag + slack, count + lag - 1):
            last = head_count if j == count + lag - 1 else done + 1
            while done < last:
                if done == 0:
                    get_windows.wait()
                arrive_halo(done)
                forward(done)
                put(0, done).start()
                put(1, done).start()
                done += 1
            if done == head_count:
                st_main[0] = stat_cols[...].T[0:16, :]
                for cond, _, copy in stat_copies():
                    when(cond, copy.start)
    for _, cond, copy in stat_copies():
        when(cond, copy.wait_recv)
    for h in range(head_count):
        arrive_halo(head_count + h)
        backward(h)
        put(2, h).start()
        put(3, h).start()

    for cond, _, copy in stat_copies():
        when(cond, copy.wait_send)
    everything = near.at[:, :, :, 1, 0:tokens, :]
    remote(everything, everything, send_sem.at[0], recv_sem.at[0, 0], (pair, sp)).wait_send()
    when(
        has_to,
        remote(everything, everything, send_sem.at[1], recv_sem.at[0, 0], (pair, sp)).wait_send,
    )
    early = near.at[:, :, :, 0:2, 0:half, :]
    late = near.at[:, :, :, 2, 0:half, :]
    for i, cond in ((2, has_up), (4, has_down)):
        when(
            cond, remote(early, early, send_sem.at[i], recv_sem.at[0, 0], (pair, sp)).wait_send
        )
        when(
            cond & has_other,
            remote(late, late, send_sem.at[i + 1], recv_sem.at[0, 0], (pair, sp)).wait_send,
        )
    for i in range(4):
        pltpu.make_async_copy(results[i][0], results[i][1], out_sem.at[i]).wait()


def put_out(*refs):
    sources, targets, held, come, go = refs[:4], refs[4:8], refs[8], refs[9], refs[10]
    ins = [pltpu.make_async_copy(sources[i], held.at[i], come.at[i]) for i in range(4)]
    outs = [pltpu.make_async_copy(held.at[i], targets[i], go.at[i]) for i in range(4)]
    for copy in ins:
        copy.start()
    for i in range(4):
        ins[i].wait()
        outs[i].start()
    for copy in outs:
        copy.wait()


def on_device(queries, key_vectors, values, grad_out, windows):
    local_shape = queries.shape
    row_count, col_count, features = local_shape[1:]
    head_count = windows.shape[1]
    head_size = features // head_count
    tokens = row_count * col_count
    sizes = (
        head_count,
        head_size,
        row_count,
        col_count,
        lax.axis_size("tm"),
        lax.axis_size("space"),
    )
    flat = (tokens, features)
    count = 2 * head_count
    outs = pl.pallas_call(
        functools.partial(kernel, sizes),
        out_shape=[jax.ShapeDtypeStruct(flat, jnp.bfloat16)] * 4,
        in_specs=[pl.BlockSpec(memory_space=pl.ANY)] * 5,
        out_specs=[pl.BlockSpec(memory_space=pl.ANY)] * 4,
        scratch_shapes=[
            pltpu.SMEM((2, head_count), jnp.int32),
            pltpu.VMEM(flat, jnp.bfloat16),
            pltpu.VMEM(flat, jnp.bfloat16),
            pltpu.VMEM(flat, jnp.bfloat16),
            pltpu.VMEM(flat, jnp.bfloat16),
            pltpu.VMEM((2, head_count, 2, 3, 2 * tokens, head_size), jnp.bfloat16),
            pltpu.VMEM((tokens, tokens), jnp.float32),
            pltpu.VMEM((3, 16, tokens), jnp.float32),
            pltpu.VMEM((3, 16, tokens), jnp.float32),
            pltpu.VMEM((3, 16, tokens), jnp.float32),
            pltpu.SemaphoreType.DMA((count + 1,)),
            pltpu.SemaphoreType.DMA((6,)),
            pltpu.SemaphoreType.DMA((count, 6)),
            pltpu.SemaphoreType.DMA((8,)),
            pltpu.SemaphoreType.DMA((8,)),
            pltpu.SemaphoreType.DMA((4,)),
        ],
        compiler_params=pltpu.CompilerParams(
            collective_id=0, has_side_effects=True, vmem_limit_bytes=63_000_000
        ),
    )(
        windows,
        queries.reshape(flat),
        key_vectors.reshape(flat),
        values.reshape(flat),
        grad_out.reshape(flat),
    )
    outs = pl.pallas_call(
        put_out,
        out_shape=[jax.ShapeDtypeStruct(flat, jnp.bfloat16)] * 4,
        in_specs=[pl.BlockSpec(memory_space=pl.ANY)] * 4,
        out_specs=[pl.BlockSpec(memory_space=pl.ANY)] * 4,
        scratch_shapes=[
            pltpu.VMEM((4,) + flat, jnp.bfloat16),
            pltpu.SemaphoreType.DMA((4,)),
            pltpu.SemaphoreType.DMA((4,)),
        ],
        compiler_params=pltpu.CompilerParams(vmem_limit_bytes=63_000_000),
    )(*outs)
    return tuple(out.reshape(local_shape) for out in outs)


def solution(mesh):
    spec = P("tm", "space", None, None)
    return jax.shard_map(
        on_device,
        mesh=mesh,
        in_specs=(spec, spec, spec, spec, P()),
        out_specs=(spec, spec, spec, spec),
        check_vma=False,
    )
```

time: 43.1 us -> 33.4 us (0.77)
  Pallas kernels: 42.3 us -> 32.5 us
    pallas_call x1, Pallas kernels: 40.3 us -> 30.5 us  [on_device(): pl.pallas_call(functools.partial(kernel, sizes), out_shape=[jax.ShapeDtyp...]
where the time goes in v3:
time: 33.4 us; the launch traced here: 33.1 us
  Pallas kernels  32.5 us (97%)
  between operations  0.64 us (2%)
    pallas_call x1, Pallas kernels, on_device(): pl.pallas_call(functools.partial(kernel, sizes), out_shape=[jax.ShapeDtyp...  30.5 us
    pallas_call x1, Pallas kernels, on_device(): pl.pallas_call(put_out, out_shape=[jax.ShapeDtypeStruct(flat, jnp.bfloat1...  1.96 us

profile of v3, /device:TPU:5, one launch (start us, length us, event | category | flops | bytes accessed | tf_op | source)
XLA Modules:
  0.0 33.1 jit_solution(7463733772727270307)
XLA Ops:
  0.6 30.5 %shard_map.84 = (bf16[128,768]{1,0:T(8,128)(2,1)}, bf16[128,768]{1,0:T(8,128)(2,1)}, bf16[128,768]{1,0:T(8,128)(2,1)}, bf16[128,768]{1,0:T(8,128)(2,1)}) custom-call(s32[2,6]{1,0:T(2,128)} %win_hbm.1, bf16[128,768]{1,0:T(8,128)(2,1)} %bitcast.8, bf16[128,768]{1,0:T(8,128)(2,1)} %bitcast.9, bf16[128,768]{1,0:T(8,128)(2,1)} %bitcast.10, bf16[128,768]{1,0:T(8,128)(2,1)} %bitcast.11), custom_call_target="tpu_custom_call" | custom-call | tf_op jit(solution)/shard_map/pallas_call | solution.py:432
  31.2 2.0 %shard_map.85 = (bf16[128,768]{1,0:T(8,128)(2,1)}, bf16[128,768]{1,0:T(8,128)(2,1)}, bf16[128,768]{1,0:T(8,128)(2,1)}, bf16[128,768]{1,0:T(8,128)(2,1)}) custom-call(bf16[128,768]{1,0:T(8,128)(2,1)} %get-tuple-element.12.refs_0_, bf16[128,768]{1,0:T(8,128)(2,1)} %get-tuple-element.13.refs_1_, bf16[128,768]{1,0:T(8,128)(2,1)} %get-tuple-element.14.refs_2_, ...), custom_call_target="tpu_custom_call" | custom-call | tf_op jit(solution)/shard_map/pallas_call | solution.py:465

commit v4 on v3

--- a/solution.py
+++ b/solution.py
@@ -27,15 +27,11 @@
     k_ref,
     v_ref,
     g_ref,
-    att_out,
-    gq_out,
-    gk_out,
-    gv_out,
-    win_ref,
     att_ref,
     gq_ref,
     gk_ref,
     gv_ref,
+    win_ref,
     near,
     stat_cols,
     st_main,
@@ -46,7 +42,6 @@
     recv_sem,
     stat_send,
     stat_recv,
-    out_sem,
 ):
     head_count, head_size, row_count, col_count, n_tm, n_space = sizes
     tokens = row_count * col_count
@@ -339,14 +334,6 @@
     stat_cols[...] = jnp.zeros_like(stat_cols)
     lag = 3
     slack = 2
-    results = ((att_ref, att_out), (gq_ref, gq_out), (gk_ref, gk_out), (gv_ref, gv_out))
-
-    def put(i, h):
-        cols = slice(h * head_size, (h + 1) * head_size)
-        return pltpu.make_async_copy(
-            results[i][0].at[:, cols], results[i][1].at[:, cols], out_sem.at[i]
-        )
-
     for h in range(head_count):
         load_wait(head_count + h)
 
@@ -363,8 +350,6 @@
                     get_windows.wait()
                 arrive_halo(done)
                 forward(done)
-                put(0, done).start()
-                put(1, done).start()
                 done += 1
             if done == head_count:
                 st_main[0] = stat_cols[...].T[0:16, :]
@@ -375,8 +360,6 @@
     for h in range(head_count):
         arrive_halo(head_count + h)
         backward(h)
-        put(2, h).start()
-        put(3, h).start()
 
     for cond, _, copy in stat_copies():
         when(cond, copy.wait_send)
@@ -396,20 +379,14 @@
             cond & has_other,
             remote(late, late, send_sem.at[i + 1], recv_sem.at[0, 0], (pair, sp)).wait_send,
         )
-    for i in range(4):
-        pltpu.make_async_copy(results[i][0], results[i][1], out_sem.at[i]).wait()
 
 
 def put_out(*refs):
-    sources, targets, held, come, go = refs[:4], refs[4:8], refs[8], refs[9], refs[10]
-    ins = [pltpu.make_async_copy(sources[i], held.at[i], come.at[i]) for i in range(4)]
-    outs = [pltpu.make_async_copy(held.at[i], targets[i], go.at[i]) for i in range(4)]
-    for copy in ins:
+    sources, targets, sems = refs[:4], refs[4:8], refs[8]
+    copies = [pltpu.make_async_copy(sources[i], targets[i], sems.at[i]) for i in range(4)]
+    for copy in copies:
         copy.start()
-    for i in range(4):
-        ins[i].wait()
-        outs[i].start()
-    for copy in outs:
+    for copy in copies:
         copy.wait()
 
 
@@ -433,13 +410,9 @@
         functools.partial(kernel, sizes),
         out_shape=[jax.ShapeDtypeStruct(flat, jnp.bfloat16)] * 4,
         in_specs=[pl.BlockSpec(memory_space=pl.ANY)] * 5,
-        out_specs=[pl.BlockSpec(memory_space=pl.ANY)] * 4,
+        out_specs=[pl.BlockSpec(memory_space=pltpu.VMEM)] * 4,
         scratch_shapes=[
             pltpu.SMEM((2, head_count), jnp.int32),
-            pltpu.VMEM(flat, jnp.bfloat16),
-            pltpu.VMEM(flat, jnp.bfloat16),
-            pltpu.VMEM(flat, jnp.bfloat16),
-            pltpu.VMEM(flat, jnp.bfloat16),
             pltpu.VMEM((2, head_count, 2, 3, 2 * tokens, head_size), jnp.bfloat16),
             pltpu.VMEM((tokens, tokens), jnp.float32),
             pltpu.VMEM((3, 16, tokens), jnp.float32),
@@ -450,10 +423,9 @@
             pltpu.SemaphoreType.DMA((count, 6)),
             pltpu.SemaphoreType.DMA((8,)),
             pltpu.SemaphoreType.DMA((8,)),
-            pltpu.SemaphoreType.DMA((4,)),
         ],
         compiler_params=pltpu.CompilerParams(
-            collective_id=0, has_side_effects=True, vmem_limit_bytes=63_000_000
+            collective_id=0, has_side_effects=True, vmem_limit_bytes=55_600_000
         ),
     )(
         windows,
@@ -465,14 +437,12 @@
     outs = pl.pallas_call(
         put_out,
         out_shape=[jax.ShapeDtypeStruct(flat, jnp.bfloat16)] * 4,
-        in_specs=[pl.BlockSpec(memory_space=pl.ANY)] * 4,
-        out_specs=[pl.BlockSpec(memory_space=pl.ANY)] * 4,
+        in_specs=[pl.BlockSpec(memory_space=pltpu.VMEM)] * 4,
+        out_specs=[pl.BlockSpec(memory_space=pltpu.HBM)] * 4,
         scratch_shapes=[
-            pltpu.VMEM((4,) + flat, jnp.bfloat16),
-            pltpu.SemaphoreType.DMA((4,)),
             pltpu.SemaphoreType.DMA((4,)),
         ],
-        compiler_params=pltpu.CompilerParams(vmem_limit_bytes=63_000_000),
+        compiler_params=pltpu.CompilerParams(vmem_limit_bytes=4_000_000),
     )(*outs)
     return tuple(out.reshape(local_shape) for out in outs)
 

time: 33.4 us -> 32.4 us (0.970)
  Pallas kernels: 32.5 us -> 30.8 us
  local copies, waits for them, and re-layouts: 0 us -> 0.67 us
    pallas_call x1, Pallas kernels: 1.96 us -> 0.91 us  [on_device(): pl.pallas_call(put_out, out_shape=[jax.ShapeDtypeStruct(flat, jnp.bfloat1...]
    pallas_call x1, Pallas kernels: 30.5 us -> 29.9 us  [on_device(): pl.pallas_call(functools.partial(kernel, sizes), out_shape=[jax.ShapeDtyp...]
    unnamed x0 -> x2, local copies, waits for them, and re-layouts: none -> 0.67 us
where the time goes in v4:
time: 32.4 us; the launch traced here: 32.1 us
  Pallas kernels  30.8 us (95%)
  local copies, waits for them, and re-layouts  0.67 us (2%)
  between operations  0.65 us (2%)
    pallas_call x1, Pallas kernels, on_device(): pl.pallas_call(functools.partial(kernel, sizes), out_shape=[jax.ShapeDtyp...  29.9 us
    pallas_call x1, Pallas kernels, on_device(): pl.pallas_call(put_out, out_shape=[jax.ShapeDtypeStruct(flat, jnp.bfloat1...  0.91 us
    unnamed x2, local copies, waits for them, and re-layouts  0.67 us

profile of v4, /device:TPU:5, one launch (start us, length us, event | category | flops | bytes accessed | tf_op | source)
XLA Modules:
  0.0 32.1 jit_solution(4713910599167528217)
XLA Ops:
  0.6 0.0 copy-start
  0.6 0.7 %copy-done = s32[2,6]{1,0:T(2,128)S(1)} copy-done((s32[2,6]{1,0:T(2,128)S(1)}, s32[2,6]{1,0:T(2,128)}, u32[]{:S(2)}) %copy-start) | copy-done | bytes 72
  1.3 29.9 %shard_map.84 = (bf16[128,768]{1,0:T(8,128)(2,1)S(1)}, bf16[128,768]{1,0:T(8,128)(2,1)S(1)}, bf16[128,768]{1,0:T(8,128)(2,1)S(1)}, bf16[128,768]{1,0:T(8,128)(2,1)S(1)}) custom-call(s32[2,6]{1,0:T(2,128)S(1)} %copy-done, bf16[128,768]{1,0:T(8,128)(2,1)} %bitcast.8, bf16[128,768]{1,0:T(8,128)(2,1)} %bitcast.9, bf16[128,768]{1,0:T(8,128)(2,1)} %bitcast.10, ...), custom_call_target="tpu_custom_call" | custom-call | tf_op jit(solution)/shard_map/pallas_call | solution.py:409
  31.2 0.9 %shard_map.85 = (bf16[128,768]{1,0:T(8,128)(2,1)}, bf16[128,768]{1,0:T(8,128)(2,1)}, bf16[128,768]{1,0:T(8,128)(2,1)}, bf16[128,768]{1,0:T(8,128)(2,1)}) custom-call(bf16[128,768]{1,0:T(8,128)(2,1)S(1)} %get-tuple-element.12.refs_0_, bf16[128,768]{1,0:T(8,128)(2,1)S(1)} %get-tuple-element.13.refs_1_, bf16[128,768]{1,0:T(8,128)(2,1)S(1)} %get-tuple-element.14.refs_2_, ...), custom_call_target="tpu_custom_call" | custom-call | tf_op jit(solution)/shard_map/pallas_call | solution.py:437
Async XLA Ops:
  0.6 0.7 %copy-start = (s32[2,6]{1,0:T(2,128)S(1)}, s32[2,6]{1,0:T(2,128)}, u32[]{:S(2)}) copy-start(s32[2,6]{1,0:T(2,128)} %win_hbm.1) | copy-start | bytes 148
